TPU v7x, 32 devices: a whole 2x2x4 slice. The times are simulated.
32 devices in a mesh: fsdp: 4 (over y, x), ctx: 4 (over z), tp: 2 (over core).
Axes of the slice: x: 2, y: 2, z: 4, core: 2. Of those that a mesh axis runs over, the one named last changes fastest.
Arguments:
- inputs: bfloat16 [3, 1024, 4, 1024], P(None, 'ctx', 'fsdp'), may hold values from -8 to 8
- block_order: int32 [3, 4, 4], P(None, 'fsdp'), may hold values from 0 to 3, each once within a row
- first_gain: bfloat16 [1024], replicated, may hold values from 0.5 to 1.5
- first_shift: bfloat16 [1024], replicated, may hold values from -1.25 to 1.25
- second_gain: bfloat16 [1024], replicated, may hold values from 0.5 to 1.5
- second_shift: bfloat16 [1024], replicated, may hold values from -1.25 to 1.25
- qkv_weight: bfloat16 [3, 1024, 1024], P(None, ('fsdp', 'ctx'), 'tp'), may hold values from -0.1875 to 0.1875
- qkv_bias: bfloat16 [3, 1024], P(None, 'tp'), may hold values from -1.25 to 1.25
- out_weight: bfloat16 [1024, 1024], P('tp', ('fsdp', 'ctx')), may hold values from -5 to 5
- out_bias: bfloat16 [1024], replicated, may hold values from -1.25 to 1.25
- up_weight: bfloat16 [1024, 4096], P(('fsdp', 'ctx'), 'tp'), may hold values from -0.1875 to 0.1875
- up_bias: bfloat16 [4096], P('tp'), may hold values from -1.25 to 1.25
- down_weight: bfloat16 [4096, 1024], P('tp', ('fsdp', 'ctx')), may hold values from -0.09375 to 0.09375
- down_bias: bfloat16 [1024], replicated, may hold values from -1.25 to 1.25
- out_grad: bfloat16 [3, 1024, 4, 1024], P(None, 'ctx', 'fsdp'), may hold values from -8 to 8
Outputs:
- outputs: bfloat16 [3, 1024, 4, 1024], P(None, 'ctx', 'fsdp')
- input_grad: bfloat16 [3, 1024, 4, 1024], P(None, 'ctx', 'fsdp')
- first_gain_grad: float32 [1024], replicated
- first_shift_grad: float32 [1024], replicated
- second_gain_grad: float32 [1024], replicated
- second_shift_grad: float32 [1024], replicated
- qkv_weight_grad: float32 [3, 1024, 1024], P(None, ('fsdp', 'ctx'), 'tp')
- qkv_bias_grad: float32 [3, 1024], P(None, 'tp')
- out_weight_grad: float32 [1024, 1024], P('tp', ('fsdp', 'ctx'))
- out_bias_grad: float32 [1024], replicated
- up_weight_grad: float32 [1024, 4096], P(('fsdp', 'ctx'), 'tp')
- up_bias_grad: float32 [4096], P('tp')
- down_weight_grad: float32 [4096, 1024], P('tp', ('fsdp', 'ctx'))
- down_bias_grad: float32 [1024], replicated
Inputs may be any that keep to these rules, and one draw needn't show every extreme that they name: block_order[m, s, c] is the position block of the tokens at rows c * 256 to (c + 1) * 256 - 1 of sequence s of micro-batch m; each row names every block once.
All inputs are finite; a program needn't handle non-finite values.
Results may differ from a plain program's by a relative error of at most 0.014.
Values may be sent and summed in bfloat16 or wider, within the bound.
No kernel may reach another device: no remote copies, remote signals or barrier semaphores. Data moves between devices by JAX's collectives and lax.ppermute only.
A program may use at most 192 MiB of HBM per device.

v0:
```python
import math

import jax
import jax.numpy as jnp
from jax import lax
from jax.experimental import pallas as pl
from jax.experimental.pallas import tpu as pltpu
from jax.sharding import PartitionSpec as P

HD = 64
ROT = 16
LANES = 128
F32 = jnp.float32
BF16 = jnp.bfloat16
MIB = 1024 * 1024
EPSILON = 1e-05
TASKS = (
    "finish_a",
    "weights_a",
    "forward_first",
    "finish_b",
    "weights_b",
    "sums",
    "forward_second",
    "attention_first",
    "totals",
    "close",
)
SMALL_ROWS = 16
SHARE = 1 / 0.6


def swap(value, axis, bit):
    size = lax.axis_size(axis)
    return lax.ppermute(value, axis, [(i, i ^ bit) for i in range(size)])


def choose(bit, first, second):
    return jnp.where(bit == 0, first, second), jnp.where(bit == 0, second, first)


def gather_column(own, other):
    return [own] + [swap(other if j & 1 else own, "ctx", j) for j in range(1, lax.axis_size("ctx"))]


def gather_pieces(column):
    return [column] + [swap(column, "fsdp", j) for j in range(1, lax.axis_size("fsdp"))]


def launch(kernel, scalars, operands, waits, us, *, grid, in_specs, out_specs, out_shape, scratch_shapes=(), mib=24, **more):
    count = (scalars is not None) + len(operands)

    def body(*refs):
        kernel(*refs[:count], *refs[count + len(waits) :])

    return pl.pallas_call(
        body,
        out_shape=out_shape,
        grid_spec=pltpu.PrefetchScalarGridSpec(
            num_scalar_prefetch=0 if scalars is None else 1,
            grid=grid,
            in_specs=[*in_specs] + [pl.BlockSpec(memory_space=pl.ANY)] * len(waits),
            out_specs=out_specs,
            scratch_shapes=scratch_shapes,
        ),
        compiler_params=pltpu.CompilerParams(vmem_limit_bytes=mib * MIB),
        cost_estimate=pl.CostEstimate(flops=int(us * SHARE * 1.1e9), bytes_accessed=1024, transcendentals=0),
        **more,
    )(*([] if scalars is None else [scalars]), *operands, *waits)


def matmul(lhs, rhs):
    return jnp.dot(lhs, rhs, preferred_element_type=F32)


def against(lhs, rhs):
    return lax.dot_general(lhs, rhs, (((1,), (1,)), ((), ())), preferred_element_type=F32)


def exchanged(load, width, index, rows):
    shift = index * rows
    high, low = shift // LANES, lax.rem(shift, LANES)
    blocks = []
    for block in range(width // LANES):
        start = pl.multiple_of((block ^ high) * LANES, LANES)
        value = load(pl.ds(start, LANES)).astype(F32)
        step = rows
        while step < LANES:
            lane = lax.broadcasted_iota(jnp.int32, value.shape, 1)
            turned = pltpu.roll(value, step, 1)
            if 2 * step != LANES:
                turned = jnp.where((lane & step) != 0, turned, pltpu.roll(value, LANES - step, 1))
            value = jnp.where((low & step) != 0, turned, value)
            step *= 2
        blocks.append(value)
    return jnp.concatenate(blocks, axis=1)


def normal_of(values):
    centre = jnp.mean(values, axis=-1, keepdims=True)
    offset = values - centre
    spread = lax.rsqrt(jnp.mean(offset * offset, axis=-1, keepdims=True) + EPSILON)
    return offset * spread, spread


def prepare_block(rows, index, load_x, load_g, gains_ref, outs):
    x_out, g_out, one_out = outs
    width = x_out.shape[1]
    values = exchanged(load_x, width, index, rows)
    gains = exchanged(lambda lanes: gains_ref[:, lanes], width, index, rows)
    normal, _ = normal_of(values)
    x_out[...] = values.astype(BF16)
    g_out[...] = exchanged(load_g, width, index, rows).astype(BF16)
    one_out[...] = (normal * gains[0:1] + gains[1:2]).astype(BF16)


def prepare_own_kernel(rows, index_ref, x_ref, g_ref, gains_ref, *refs):
    outs, sum_out = refs[:3], refs[3]
    prepare_block(rows, index_ref[0], lambda lanes: x_ref[:, lanes], lambda lanes: g_ref[:, lanes], gains_ref, outs)

    @pl.when(pl.program_id(0) == 0)
    def _():
        sum_out[...] = jnp.zeros_like(sum_out)

    sum_out[...] += jnp.sum(g_ref[...].astype(F32), axis=0, keepdims=True)


def prepare_pair_kernel(rows, count, index_ref, mine_ref, other_ref, gains_ref, *refs):
    half = mine_ref.shape[2]

    def loader(field):
        def load(lanes):
            inside = pl.ds(pl.multiple_of(lax.rem(lanes.start, half), LANES), lanes.size)
            mine, other = mine_ref[field, :, inside].astype(F32), other_ref[field, :, inside].astype(F32)
            return jnp.where(lanes.start // half == index_ref[1], mine, other)

        return load

    own_refs, out_refs = refs[:3], refs[3:]
    step = pl.program_id(0)

    @pl.when(step < count)
    def _():
        for own, out in zip(own_refs, out_refs):
            out[...] = own[...]

    @pl.when(step >= count)
    def _():
        prepare_block(rows, index_ref[0], loader(0), loader(1), gains_ref, out_refs)


def prepare_late_kernel(rows, index_ref, x_ref, g_ref, one_ref, gains_ref, two_out, one_t, two_t, g_t):
    normal, _ = normal_of(x_ref[...].astype(F32))
    gains = exchanged(lambda lanes: gains_ref[:, lanes], x_ref.shape[1], index_ref[0], rows)
    two = (normal * gains[2:3] + gains[3:4]).astype(BF16)
    two_out[...] = two
    one_t[...] = one_ref[...].T
    two_t[...] = two.T
    g_t[...] = g_ref[...].T


def prepare_own(index, x, g, gains, rows, block_rows, waits=()):
    tokens, width = x.shape
    row_spec = pl.BlockSpec((block_rows, width), lambda m, *_: (m, 0))
    *outs, grad_sum = launch(
        lambda *refs: prepare_own_kernel(rows, *refs),
        index,
        [x, g, gains],
        waits,
        2.100,
        out_shape=[jax.ShapeDtypeStruct((tokens, width), BF16)] * 3 + [jax.ShapeDtypeStruct((1, width), F32)],
        grid=(tokens // block_rows,),
        in_specs=[row_spec, row_spec, pl.BlockSpec(gains.shape, lambda m, *_: (0, 0))],
        out_specs=[row_spec] * 3 + [pl.BlockSpec((1, width), lambda m, *_: (0, 0))],
        name="prepare_own",
    )
    return outs, grad_sum


def prepare_pair(index, arrived, gains, own, rows, block_rows, first_part, waits=()):
    _, tokens, half = arrived[0].shape
    width = 2 * half
    count = tokens // block_rows

    def place(step):
        m, side = lax.rem(step, count), step // count
        return m + jnp.where(m < first_part, side * first_part, first_part + side * (count - first_part))

    half_spec = pl.BlockSpec((2, block_rows, half), lambda m, *_: (0, jnp.maximum(m - count, 0), 0))
    own_spec = pl.BlockSpec((block_rows, width), lambda m, *_: (jnp.minimum(m, count - 1), 0))
    return launch(
        lambda *refs: prepare_pair_kernel(rows, count, *refs),
        index,
        [*arrived, gains, *own],
        waits,
        2.100,
        out_shape=[jax.ShapeDtypeStruct((2 * tokens, width), BF16)] * 3,
        grid=(2 * count,),
        in_specs=[half_spec, half_spec, pl.BlockSpec(gains.shape, lambda m, *_: (0, 0))] + [own_spec] * 3,
        out_specs=[pl.BlockSpec((block_rows, width), lambda m, *_: (place(m), 0))] * 3,
        name="prepare_pair",
    )


def prepare_late(index, x, g, one, gains, rows, block_rows, waits=()):
    tokens, width = x.shape
    row_spec = pl.BlockSpec((block_rows, width), lambda m, *_: (m, 0))
    column_spec = pl.BlockSpec((width, block_rows), lambda m, *_: (0, m))
    plain, turned = jax.ShapeDtypeStruct((tokens, width), BF16), jax.ShapeDtypeStruct((width, tokens), BF16)
    return launch(
        lambda *refs: prepare_late_kernel(rows, *refs),
        index,
        [x, g, one, gains],
        waits,
        3.600,
        out_shape=[plain, turned, turned, turned],
        grid=(tokens // block_rows,),
        in_specs=[row_spec, row_spec, row_spec, pl.BlockSpec(gains.shape, lambda m, *_: (0, 0))],
        out_specs=[row_spec, column_spec, column_spec, column_spec],
        name="prepare_late",
        mib=24,
    )


def turn(values, cosine, sine):
    lane = lax.broadcasted_iota(jnp.int32, values.shape, 1) % HD
    ahead = pltpu.roll(values, LANES - ROT // 2, 1)
    behind = pltpu.roll(values, ROT // 2, 1)
    return values * cosine + jnp.where(lane < ROT // 2, ahead, behind) * sine


def gather_weight(piece_refs, weight_s):
    @pl.when(pl.program_id(0) == 0)
    def _():
        start = 0
        for ref in piece_refs:
            weight_s[start : start + ref.shape[0], :] = ref[...]
            start += ref.shape[0]


def pick(place, first, second):
    return jnp.where(place == 0, first, second), jnp.where(place == 0, second, first)


def project_kernel(fsdp, block_rows, scalar_ref, one_ref, g_ref, table_ref, bias_ref, *refs):
    piece_refs, (local_ref, remote_ref, weight_s) = refs[:fsdp], refs[fsdp:]
    tokens, width = one_ref.shape
    gather_weight(piece_refs, weight_s)
    pre = matmul(one_ref[...], weight_s[:, : 6 * LANES]) + bias_ref[...]
    back = matmul(g_ref[...], weight_s[:, 6 * LANES :])
    for block in range(tokens // block_rows):
        rows = slice(block * block_rows, (block + 1) * block_rows)
        rank = scalar_ref[1 + pl.program_id(0) * (tokens // block_rows) + block]
        places = pl.ds(pl.multiple_of(rank * block_rows, block_rows), block_rows)
        cosine, sine = table_ref[0, places, :], table_ref[1, places, :]
        for field in range(4):
            source = pre[rows] if field < 3 else back[rows]
            start = 2 * field * LANES if field < 3 else 0
            both = [source[:, start + group * LANES : start + (group + 1) * LANES] for group in range(2)]
            if field < 2:
                both = [turn(item, cosine, sine) for item in both]
            here = slice(field * LANES, (field + 1) * LANES)
            mine, other = pick(scalar_ref[0], *both)
            local_ref[rows, here] = mine.astype(BF16)
            remote_ref[rows, here] = other.astype(BF16)


def project(place, ranks, one, g, first, count, table, bias, pieces, block_rows, waits=()):
    width = one.shape[1]
    fsdp = len(pieces)
    tokens = count * block_rows
    tile = 2 * block_rows
    base = first // 2
    side = pl.BlockSpec((tile, width), lambda t, *_: (base + t, 0))
    once = pl.Buffered(1)
    out = pl.BlockSpec((tile, 4 * LANES), lambda t, *_: (t, 0))
    return launch(
        lambda *refs: project_kernel(fsdp, block_rows, *refs),
        jnp.concatenate([place, ranks]),
        [one, g, table, bias, *pieces],
        waits,
        tokens / 500.000,
        out_shape=[jax.ShapeDtypeStruct((tokens, 4 * LANES), BF16)] * 2,
        grid=(tokens // tile,),
        in_specs=[
            side,
            side,
            pl.BlockSpec(table.shape, lambda t, *_: (0, 0, 0), pipeline_mode=once),
            pl.BlockSpec(bias.shape, lambda t, *_: (0, 0)),
        ]
        + [pl.BlockSpec(piece.shape, lambda t, *_: (0, 0), pipeline_mode=once) for piece in pieces],
        out_specs=[out, out],
        scratch_shapes=[pltpu.VMEM((width, 8 * LANES), BF16)],
        name="project",
        mib=28,
    )


def attend_kernel(blocks, block_rows, scale, rank_ref, table_ref, *refs):
    count = blocks // 2
    chunk_refs, out_refs = refs[:count], refs[count : 2 * count]
    q_s, k_s, v_s, d_s, kt_s, vt_s, ot_s, qt_s, dk_s, dv_s = refs[2 * count :]
    item = pl.program_id(0)

    def rows_of(index):
        return pl.ds(pl.multiple_of(rank_ref[item * blocks + index] * block_rows, block_rows), block_rows)

    for index in range(blocks):
        rows, chunk, side = rows_of(index), chunk_refs[index // 2], index % 2
        q_s[rows, :] = chunk[side, 0, :, :LANES]
        k_s[rows, :] = chunk[side, 0, :, LANES : 2 * LANES]
        v_s[rows, :] = chunk[side, 0, :, 2 * LANES : 3 * LANES]
        d_s[rows, :] = chunk[side, 0, :, 3 * LANES :]
    kt_s[...] = k_s[...].T
    vt_s[...] = v_s[...].T
    lane = lax.broadcasted_iota(jnp.int32, (block_rows, LANES), 1)
    dk_s[...] = jnp.zeros_like(dk_s)
    dv_s[...] = jnp.zeros_like(dv_s)

    def head_step(head, carry):
        inside = (lane // HD) == head
        heads = pl.ds(pl.multiple_of(head * HD, HD), HD)
        for rank in range(blocks):
            rows = slice(rank * block_rows, (rank + 1) * block_rows)
            keys = slice(0, (rank + 1) * block_rows)
            q_h = jnp.where(inside, q_s[rows, :], 0).astype(BF16)
            d_h = jnp.where(inside, d_s[rows, :], 0).astype(BF16)
            scores = against(k_s[keys, :], q_h) * scale
            weights = jnp.exp(scores - jnp.max(scores, axis=0, keepdims=True))
            weights = weights * (1.0 / jnp.sum(weights, axis=0, keepdims=True))
            low = weights.astype(BF16)
            ot_s[heads, rows] = matmul(vt_s[heads, keys], low)
            dv_s[keys, :] += matmul(low, d_h)
            slope = against(v_s[keys, :], d_h)
            delta = jnp.sum(weights * slope, axis=0, keepdims=True)
            slope = (weights * (slope - delta)).astype(BF16)
            qt_s[heads, rows] = matmul(kt_s[heads, keys], slope)
            dk_s[keys, :] += matmul(slope, q_h)
        return carry

    lax.fori_loop(0, LANES // HD, head_step, 0)
    for index in range(blocks):
        rows, out, side = rows_of(index), out_refs[index // 2], index % 2
        cosine, sine = table_ref[0, rows, :], -table_ref[1, rows, :]
        out[side, 0, :, :LANES] = turn(qt_s[:, rows].T * scale, cosine, sine).astype(BF16)
        out[side, 0, :, LANES : 2 * LANES] = turn(dk_s[rows, :] * scale, cosine, sine).astype(BF16)
        out[side, 0, :, 2 * LANES : 3 * LANES] = dv_s[rows, :].astype(BF16)
        out[side, 0, :, 3 * LANES :] = ot_s[:, rows].T.astype(BF16)


def attend(ranks, table, chunks, waits=()):
    sides, count, block_rows, _ = chunks[0].shape
    blocks = sides * len(chunks)
    length = blocks * block_rows
    spec = pl.BlockSpec((sides, 1, block_rows, 4 * LANES), lambda m, *_: (0, m, 0, 0))
    pairs = count * blocks * (blocks + 1) // 2 * block_rows * block_rows
    return launch(
        lambda *refs: attend_kernel(blocks, block_rows, HD ** (-0.5), *refs),
        ranks,
        [table, *chunks],
        waits,
        11 * count,
        out_shape=[jax.ShapeDtypeStruct(chunk.shape, BF16) for chunk in chunks],
        grid=(count,),
        in_specs=[pl.BlockSpec(table.shape, lambda m, *_: (0, 0, 0))] + [spec] * len(chunks),
        out_specs=[spec] * len(chunks),
        scratch_shapes=[pltpu.VMEM((length, LANES), BF16)] * 4
        + [pltpu.VMEM((LANES, length), BF16)] * 2
        + [pltpu.VMEM((LANES, length), F32)] * 2
        + [pltpu.VMEM((length, LANES), F32)] * 2,
        name="attend",
        mib=24,
    )


def forward_kernel(fsdp, two_ref, g_ref, two_t, g_t, bias_ref, *refs):
    up_refs, down_refs = refs[:fsdp], refs[fsdp : 2 * fsdp]
    branch_ref, slope_ref, sum_ref = refs[2 * fsdp : 2 * fsdp + 3]
    out_refs, (up_s, down_s) = refs[2 * fsdp + 3 : -2], refs[-2:]
    width = two_ref.shape[1]
    span = width // fsdp
    lanes = [slice(offset * span, (offset + 1) * span) for offset in range(fsdp)]
    for offset in range(fsdp):
        up_s[lanes[offset], :] = up_refs[offset][...]
        down_s[lanes[offset], :] = down_refs[offset][...]
    pre = matmul(two_ref[...], up_s[...]) + bias_ref[...]
    back = matmul(g_ref[...], down_s[...])
    gate = 0.5 * (1.0 + lax.erf(pre * math.sqrt(0.5)))
    bell = jnp.exp(-0.5 * pre * pre) * (1.0 / math.sqrt(2.0 * math.pi))
    hidden = (pre * gate).astype(BF16)
    pre_grad = (back * (gate + pre * bell)).astype(BF16)
    sum_ref[...] = jnp.sum(pre_grad.astype(F32), axis=0, keepdims=True)

    @pl.when(pl.program_id(0) == 0)
    def _():
        branch_ref[...] = against(hidden, down_s[...])
        slope_ref[...] = against(pre_grad, up_s[...])

    @pl.when(pl.program_id(0) != 0)
    def _():
        branch_ref[...] += against(hidden, down_s[...])
        slope_ref[...] += against(pre_grad, up_s[...])

    for offset in range(fsdp):
        out = out_refs[offset]
        out[0] = matmul(two_t[lanes[offset], :], pre_grad).astype(out.dtype)
        out[1] = matmul(g_t[lanes[offset], :], hidden).astype(out.dtype)


def feed_forward(two, g, two_t, g_t, bias, pieces, waits=()):
    tokens, width = two.shape
    fsdp = len(pieces)
    span, hidden = pieces[0].shape[0], pieces[0].shape[1] // 2
    tile = 512
    tiles = hidden // tile
    once = pl.Buffered(1)
    whole = pl.BlockSpec((tokens, width), lambda n: (0, 0), pipeline_mode=once)
    whole_t = pl.BlockSpec((width, tokens), lambda n: (0, 0), pipeline_mode=once)
    piece = pl.BlockSpec((span, tile), lambda n: (0, n))
    later = pl.BlockSpec((span, tile), lambda n: (0, n + tiles))
    line = pl.BlockSpec((1, tile), lambda n: (0, n))
    grads = [jax.ShapeDtypeStruct((2, span, hidden), BF16 if offset else F32) for offset in range(fsdp)]
    grad = pl.BlockSpec((2, span, tile), lambda n: (0, 0, n))
    branch, slope, sums, *grads = launch(
        lambda *refs: forward_kernel(fsdp, *refs),
        None,
        [two, g, two_t, g_t, bias, *pieces, *pieces],
        waits,
        34,
        out_shape=[jax.ShapeDtypeStruct((tokens, width), F32)] * 2
        + [jax.ShapeDtypeStruct((1, hidden), F32)]
        + grads,
        grid=(tiles,),
        in_specs=[whole, whole, whole_t, whole_t, line] + [piece] * fsdp + [later] * fsdp,
        out_specs=[whole, whole, line] + [grad] * fsdp,
        scratch_shapes=[pltpu.VMEM((width, tile), BF16)] * 2,
        name="feed_forward",
        mib=60,
    )
    return branch, slope, sums, grads


def collect(place, local_ref, remote_ref, stack_s):
    for ref, group in ((local_ref, place), (remote_ref, 1 - place)):
        for field in range(4):
            here = pl.ds(pl.multiple_of((2 * field + group) * LANES, LANES), LANES)
            stack_s[:, here] = ref[:, field * LANES : (field + 1) * LANES]


def weights_kernel(fsdp, last, place_ref, one_t, g_t, local_ref, remote_ref, *refs):
    before_ref, small_ref = refs[:2] if last else (None, None)
    out_refs, stack_s = refs[2 if last else 0 : -1], refs[-1]
    step = pl.program_id(0)
    span = one_t.shape[0]

    @pl.when(step == 0)
    def _():
        collect(place_ref[0], local_ref, remote_ref, stack_s)

    pre_part = matmul(one_t[...], stack_s[:, : 6 * LANES])
    out_part = matmul(g_t[...], stack_s[:, 6 * LANES :])
    if not last:
        out_refs[0][0, :, : 6 * LANES] = pre_part
        out_refs[0][0, :, 6 * LANES :] = out_part
    else:
        pre_part = pre_part + before_ref[0, :, : 6 * LANES]
        out_part = out_part + before_ref[0, :, 6 * LANES :]
        small = small_ref[...].astype(BF16)
        for offset in range(fsdp):

            @pl.when(step == offset)
            def _():
                out = out_refs[offset]
                out[0, :span, : 6 * LANES] = pre_part.astype(out.dtype)
                out[0, :span, 6 * LANES :] = out_part.astype(out.dtype)
                out[0, span:, :] = small.astype(out.dtype)


def attention_weights(place, one_t, g_t, first, local, remote, before, fsdp, waits=()):
    width = one_t.shape[0]
    tokens = local.shape[0]
    span = width // fsdp
    columns = 8 * LANES
    last = before is not None
    stack = jax.ShapeDtypeStruct((fsdp, span, columns), F32)
    grads = [
        jax.ShapeDtypeStruct((1, span + SMALL_ROWS, columns), BF16 if offset else F32) for offset in range(fsdp)
    ]
    piece = pl.BlockSpec((span, tokens), lambda o, *_: (o, first // tokens))
    slab = pl.BlockSpec((1, span, columns), lambda o, *_: (o, 0, 0))
    whole = lambda item: pl.BlockSpec(item.shape, lambda o, *_: (0,) * len(item.shape))
    grads = launch(
        lambda *refs: weights_kernel(fsdp, last, *refs),
        place,
        [one_t, g_t, local, remote, *(before if last else [])],
        waits,
        7 if last else 0.5,
        out_shape=grads if last else [stack],
        grid=(fsdp,),
        in_specs=[piece, piece, whole(local), whole(remote)] + ([slab, whole(before[1])] if last else []),
        out_specs=[whole(item) for item in grads] if last else [slab],
        scratch_shapes=[pltpu.VMEM((tokens, columns), BF16)],
        name="attention_weights",
    )
    return list(grads) if last else grads[0]


def finish_kernel(fsdp, rows, scalar_ref, x_ref, gains_ref, branch_ref, slope_ref, local_ref, remote_ref, before_ref, *refs):
    piece_refs, (mine_ref, theirs_ref, small_ref, stack_s, one_s, branch_s, out_s, norm_s) = refs[:fsdp], refs[fsdp:]
    half, width = x_ref.shape
    span = width // fsdp
    step = pl.program_id(0)
    index = scalar_ref[0]
    gains = exchanged(lambda item: gains_ref[:, item], width, index, rows)

    @pl.when(step == 0)
    def _():
        norm_s[...] = jnp.zeros_like(norm_s)
        collect(scalar_ref[1], local_ref, remote_ref, stack_s)
        for offset in range(fsdp):
            lanes = slice(offset * span, (offset + 1) * span)
            one_s[:, lanes] = against(stack_s[:, : 6 * LANES], piece_refs[offset][:, : 6 * LANES])
            branch_s[:, lanes] = against(stack_s[:, 6 * LANES :], piece_refs[offset][:, 6 * LANES :])

    here = pl.ds(pl.multiple_of((2 * lax.rem(step, 2) + ((step // 2) ^ scalar_ref[3])) * half, half), half)
    one, two = one_s[here, :], slope_ref[...]
    normal, _ = normal_of(x_ref[...].astype(F32))
    norm_s[0:1, :] += jnp.sum(one * normal, axis=0, keepdims=True)
    norm_s[1:2, :] += jnp.sum(one, axis=0, keepdims=True)
    norm_s[2:3, :] += jnp.sum(two * normal, axis=0, keepdims=True)
    norm_s[3:4, :] += jnp.sum(two, axis=0, keepdims=True)
    plain = []
    for value in (branch_ref[...] + branch_s[here, :], one * gains[0:1] + two * gains[2:3]):
        out_s[...] = value
        plain.append(exchanged(lambda item: out_s[:, item], width, index, rows).astype(BF16))

    for which, ref in enumerate((mine_ref, theirs_ref)):

        @pl.when(step // 2 == which)
        def _():
            ref[0, 0], ref[0, 1] = plain

    @pl.when(step == 3)
    def _():
        small_ref[...] = before_ref[...]
        small_ref[0:4, :] += exchanged(lambda item: norm_s[0:4, item], width, index, rows)
        small_ref[pl.ds(5 + scalar_ref[2], 1), : 6 * LANES] += jnp.sum(
            stack_s[:, : 6 * LANES].astype(F32), axis=0, keepdims=True
        )


def finish(scalars, x, gains, branch, slope, first, local, remote, small, pieces, rows, waits=()):
    width = x.shape[1]
    fsdp = len(pieces)
    half = local.shape[0] // 4
    base = first // half
    once = pl.Buffered(1)
    fixed = lambda item: pl.BlockSpec(item.shape, lambda t, *_: (0, 0))
    place = lambda t, scalars: 2 * lax.rem(t, 2) + ((t // 2) ^ scalars[3])
    row_spec = pl.BlockSpec((half, width), lambda t, scalars: (base + place(t, scalars), 0))
    back_spec = pl.BlockSpec(local.shape, lambda t, *_: (0, 0), pipeline_mode=once)
    mine_spec = pl.BlockSpec((1, 2, half, width), lambda t, *_: (jnp.minimum(t, 1), 0, 0, 0))
    theirs_spec = pl.BlockSpec((1, 2, half, width), lambda t, *_: (jnp.maximum(t - 2, 0), 0, 0, 0))
    sums = jax.ShapeDtypeStruct((2, 2, half, width), BF16)
    return launch(
        lambda *refs: finish_kernel(fsdp, rows, *refs),
        scalars,
        [x, gains, branch, slope, local, remote, small, *pieces],
        waits,
        half / 20 if first else 0.5,
        out_shape=[sums, sums, jax.ShapeDtypeStruct(small.shape, F32)],
        grid=(4,),
        in_specs=[row_spec, fixed(gains), row_spec, row_spec, back_spec, back_spec, fixed(small)]
        + [pl.BlockSpec(piece.shape, lambda t, *_: (0, 0), pipeline_mode=once) for piece in pieces],
        out_specs=[mine_spec, theirs_spec, fixed(small)],
        scratch_shapes=[
            pltpu.VMEM((4 * half, 8 * LANES), BF16),
            pltpu.VMEM((4 * half, width), F32),
            pltpu.VMEM((4 * half, width), F32),
            pltpu.VMEM((half, width), F32),
            pltpu.VMEM((8, width), F32),
        ],
        name="finish",
        mib=40,
    )


def sums_kernel(parts, *refs):
    terms, out = refs[:-1], refs[-1]
    start = 0
    for number in range(parts):
        mine, other = terms[2 * number : 2 * number + 2]
        rows = slice(start, start + mine.shape[2])
        total = mine[0, 0].astype(F32) + other[0, 0].astype(F32)
        if len(terms) > 2 * parts:
            total = total + terms[-1][0, rows, :].astype(F32)
        out[0, rows, :] = total.astype(BF16)
        start += mine.shape[2]


def core_sums(side, terms, more=(), waits=(), us=2):
    fields, width = terms[0].shape[1], terms[0].shape[3]
    rows = sum(item.shape[2] for item in terms[::2])
    field = pl.BlockSpec((1, rows, width), lambda n: (n, 0, 0))
    return launch(
        lambda *refs: sums_kernel(len(terms) // 2, *refs),
        None,
        [*terms, *more],
        waits,
        us,
        out_shape=jax.ShapeDtypeStruct((fields, rows, width), BF16),
        grid=(fields,),
        in_specs=[pl.BlockSpec((1, 1, item.shape[2], width), lambda n: (side, n, 0, 0)) for item in terms]
        + [field] * len(more),
        out_specs=field,
        name="core_sums",
    )


def tree_sum(terms):
    while len(terms) > 1:
        terms = [first + second for first, second in zip(terms[::2], terms[1::2])]
    return terms[0]


def reduce_kernel(body, cuts, *refs):
    in_refs, out_refs = refs[: -len(cuts)], refs[-len(cuts) :]
    extra = in_refs[0].shape[1] - body
    for (start, count, _), out in zip(cuts, out_refs):
        rows = slice(start, start + count)
        out[0, :count, :] = tree_sum([ref[0, rows, :].astype(F32) for ref in in_refs]).astype(out.dtype)
    if extra:
        small = tree_sum([ref[0, body:, :].astype(F32) for ref in in_refs]).astype(BF16)
        for (_, count, _), out in zip(cuts, out_refs):
            out[0, count:, :] = small.astype(out.dtype)


def reduce_and_cut(terms, cuts, waits=(), extra=0, us=3):
    stacks, rows, columns = terms[0].shape
    tile = min(columns, 512)
    spec = lambda count: pl.BlockSpec((1, count, tile), lambda a, b: (a, 0, b))
    return launch(
        lambda *refs: reduce_kernel(rows - extra, cuts, *refs),
        None,
        terms,
        waits,
        us,
        out_shape=[jax.ShapeDtypeStruct((stacks, count + extra, columns), dtype) for _, count, dtype in cuts],
        grid=(stacks, columns // tile),
        in_specs=[spec(rows)] * len(terms),
        out_specs=[spec(count + extra) for _, count, _ in cuts],
        name="reduce_and_cut",
    )


def scatter(stack):
    return [stack[0]] + [swap(piece, "fsdp", j) for j, piece in enumerate(stack) if j > 0]


def close_kernel(source, core_ref, x_ref, g_ref, mine_ref, other_ref, shift_ref, out_ref, grad_ref):
    core, _ = source(pl.program_id(0))
    values = x_ref[...].astype(F32)
    normal, spread = normal_of(values)
    total, slope = (
        jnp.where(core == core_ref[0], mine_ref[field].astype(F32), other_ref[field].astype(F32)) for field in range(2)
    )
    out_ref[...] = (values + total + shift_ref[...]).astype(BF16)
    slope_mean = jnp.mean(slope, axis=-1, keepdims=True)
    slope_dot = jnp.mean(slope * normal, axis=-1, keepdims=True)
    grad_ref[...] = (g_ref[...].astype(F32) + spread * (slope - slope_mean - normal * slope_dot)).astype(BF16)


def close(core, x, g, mine, other, shift, first_rows, waits=()):
    tokens, width = x.shape
    block = math.gcd(math.gcd(first_rows // 2, (tokens - first_rows) // 2), 128)
    first, rest = first_rows // (2 * block), (tokens - first_rows) // (2 * block)

    def source(m):
        late = m >= 2 * first
        local = m - jnp.where(late, 2 * first, 0)
        count = jnp.where(late, rest, first)
        core = jnp.where(local >= count, 1, 0)
        return core, local - core * count + jnp.where(late, first, 0)

    row_spec = pl.BlockSpec((block, width), lambda m, *_: (m, 0))
    total_spec = pl.BlockSpec((2, block, width), lambda m, *_: (0, source(m)[1], 0))
    return launch(
        lambda *refs: close_kernel(source, *refs),
        core,
        [x, g, mine, other, shift],
        waits,
        3,
        out_shape=[jax.ShapeDtypeStruct((tokens, width), BF16)] * 2,
        grid=(tokens // block,),
        in_specs=[row_spec, row_spec, total_spec, total_spec, pl.BlockSpec((1, width), lambda m, *_: (0, 0))],
        out_specs=[row_spec] * 2,
        name="close",
    )


def ranks_of(order, offsets):
    sources = lax.axis_index("ctx") ^ jnp.array(offsets, dtype=jnp.int32)
    match = sources[:, None] == jnp.arange(order.shape[1], dtype=jnp.int32)[None, :]
    return jnp.sum(jnp.where(match, order[:, None, :], 0), axis=-1)


def exchange_attention(local, remote, order, table, block_rows, waits):
    shape = (2, order.shape[0], block_rows, 4 * LANES)
    ranks = ranks_of(order, range(4)).reshape(-1)
    outs = attend(ranks, table, [local.reshape(shape), remote.reshape(shape)], waits)
    mine, theirs = (out.reshape(local.shape) for out in outs)
    return mine, swap(theirs, "ctx", 2)


def gathered_attention(local, remote, order, table, block_rows, waits):
    groups, micro = 2, order.shape[0]
    ctx = lax.axis_size("ctx")
    heads = groups * LANES // HD
    scale = HD ** (-0.5)
    packed = jnp.stack([local, remote]).reshape(groups, 2, micro, block_rows, 4 * LANES)
    packed = jnp.transpose(packed, (0, 2, 1, 3, 4))
    ranks = ranks_of(order, range(ctx))

    def split(array):
        array = array.reshape(groups, 2 * block_rows, LANES // HD, HD)
        return jnp.transpose(array, (1, 0, 2, 3)).reshape(2 * block_rows, heads, HD)

    def join(array):
        return jnp.transpose(array.reshape(2, block_rows, groups, LANES), (2, 0, 1, 3))

    def everywhere(array):
        return jnp.stack([array] + [swap(array, "ctx", j) for j in range(2, ctx, 2)])

    def home(array):
        total = array[0].astype(F32)
        for j in range(2, ctx, 2):
            total = total + swap(array[j // 2], "ctx", j).astype(F32)
        return total

    results = []
    for m in range(micro):
        parted = packed[:, m].reshape(groups, 2 * block_rows, 4, LANES)
        queries, keys, values, douts = (split(parted[:, :, i]) for i in range(4))
        all_keys, all_values = everywhere(keys), everywhere(values)
        key_ranks = jnp.repeat(ranks[m].reshape(-1, 2), block_rows, axis=1)
        query_ranks = key_ranks[0]
        allowed = (key_ranks[:, None, :] <= query_ranks[None, :, None])[:, None]

        def peak_step(state, item):
            key, value, ok = item
            peak, total, sums = state
            scores = jnp.einsum("bhe,rhe->hbr", queries, key, preferred_element_type=F32) * scale
            scores = jnp.where(ok, scores, -1e30)
            new = jnp.maximum(peak, jnp.max(scores, axis=-1))
            weights = jnp.where(ok, jnp.exp(scores - new[..., None]), 0.0)
            fade = jnp.exp(peak - new)
            part = jnp.einsum("hbr,rhe->hbe", weights.astype(BF16), value, preferred_element_type=F32)
            return (new, total * fade + jnp.sum(weights, axis=-1), sums * fade[..., None] + part), None

        start = (
            jnp.full((heads, 2 * block_rows), -1e30, F32),
            jnp.zeros((heads, 2 * block_rows), F32),
            jnp.zeros((heads, 2 * block_rows, HD), F32),
        )
        (peak, total, sums), _ = lax.scan(peak_step, start, (all_keys, all_values, allowed))
        attended = jnp.transpose(sums / total[..., None], (1, 0, 2))
        level = peak + jnp.log(total)
        delta = jnp.transpose(jnp.sum(douts.astype(F32) * attended, axis=-1))

        def back_step(query_sum, item):
            key, value, ok = item
            scores = jnp.einsum("bhe,rhe->hbr", queries, key, preferred_element_type=F32) * scale
            weights = jnp.where(ok, jnp.exp(scores - level[..., None]), 0.0)
            value_grad = jnp.einsum("hbr,bhe->rhe", weights.astype(BF16), douts, preferred_element_type=F32)
            slope = jnp.einsum("bhe,rhe->hbr", douts, value, preferred_element_type=F32)
            slope = (weights * (slope - delta[..., None])).astype(BF16)
            query_part = jnp.einsum("hbr,rhe->bhe", slope, key, preferred_element_type=F32) * scale
            key_grad = jnp.einsum("hbr,bhe->rhe", slope, queries, preferred_element_type=F32) * scale
            return query_sum + query_part, (key_grad.astype(BF16), value_grad.astype(BF16))

        query_grad, (key_grads, value_grads) = lax.scan(
            back_step, jnp.zeros(queries.shape, F32), (all_keys, all_values, allowed)
        )
        rows = [
            lax.dynamic_slice(table, (0, ranks[m, side] * block_rows, 0), (2, block_rows, LANES)) for side in range(2)
        ]
        rows = jnp.concatenate(rows, axis=1)

        def unturn(array):
            half = ROT // 2
            cosine, sine = rows[0, :, :half][:, None], rows[1, :, half:ROT][:, None]
            first, second = array[..., :half], array[..., half:ROT]
            return jnp.concatenate(
                [first * cosine + second * sine, second * cosine - first * sine, array[..., ROT:]], axis=-1
            )

        fields = (unturn(query_grad), unturn(home(key_grads)), home(value_grads), attended)
        results.append(jnp.concatenate([join(field.astype(BF16)) for field in fields], axis=-1))
    results = jnp.transpose(jnp.stack(results, axis=1), (0, 2, 1, 3, 4))
    mine, theirs = results.reshape(groups, *local.shape)
    return mine, theirs


def rotation_table(length):
    lane = jnp.arange(LANES, dtype=jnp.int32) % HD
    halves = ROT // 2
    frequency = jnp.exp((lane % halves).astype(F32) * (-2.0 * math.log(10000.0) / ROT))
    frequency = jnp.where(lane < ROT, frequency, 0.0)
    angles = jnp.arange(length, dtype=F32)[:, None] * frequency
    return jnp.stack([jnp.cos(angles), jnp.where(lane < halves, -1.0, 1.0) * jnp.sin(angles)])


def local(
    inputs,
    block_order,
    first_gain,
    first_shift,
    second_gain,
    second_shift,
    qkv_weight,
    qkv_bias,
    out_weight,
    out_bias,
    up_weight,
    up_bias,
    down_weight,
    down_bias,
    out_grad,
):
    micro, block_rows, _, width = inputs.shape
    ctx = lax.axis_size("ctx")
    f, z, core = lax.axis_index("fsdp"), lax.axis_index("ctx"), lax.axis_index("tp")
    low = z & 1
    rows = up_weight.shape[0]
    groups, hidden = 2, up_weight.shape[1] // 2
    tokens = micro * block_rows
    order = block_order[:, 0]
    first_part = micro - 1
    parts = ((0, first_part), (first_part, micro))
    exchanging = ctx == 2 * groups

    fields = [qkv_weight[0], qkv_weight[1], qkv_weight[2], jnp.transpose(out_weight)]
    extent = groups * LANES
    halves = [jnp.concatenate([field[:, i * extent : (i + 1) * extent] for field in fields], axis=1) for i in range(2)]
    shard = jnp.stack(halves)

    x, g = inputs.reshape(tokens, width), out_grad.reshape(tokens, width)
    fields = [up_weight, jnp.transpose(down_weight)]
    halves = [jnp.concatenate([field[:, i * hidden : (i + 1) * hidden] for field in fields], axis=1) for i in range(2)]
    forward_shard, both, shard = lax.optimization_barrier((jnp.stack(halves), jnp.stack([x, g]), shard))
    column = gather_column(*choose(low, shard[0], shard[1]))
    own, other = choose(low, forward_shard[0], forward_shard[1])
    forward_pair = jnp.concatenate([own, swap(other, "ctx", 1)], axis=0)
    lanes, _ = choose(core, both[:, :, : width // 2], both[:, :, width // 2 :])
    lanes, column[1] = lax.optimization_barrier((lanes, column[1]))
    lanes = swap(lanes, "ctx", 1)
    column = jnp.concatenate(column, axis=0)
    pieces = gather_pieces(column)

    table = rotation_table(ctx * block_rows)
    index = jnp.stack([f * ctx + z, core]).astype(jnp.int32)
    gains = jnp.stack([first_gain, first_shift, second_gain, second_shift]).astype(F32)
    prepared, grad_sum = prepare_own(
        index, x, g, gains, rows, block_rows, (column, forward_pair, table)
    )
    forward_column = [forward_pair] + [swap(forward_pair, "ctx", j) for j in range(2, ctx, 2)]
    lanes, grad_sum, *pieces = lax.optimization_barrier((lanes, grad_sum, *pieces))
    arrived = (lanes, swap(lanes, "tp", 1))
    x_both, g_both, one = prepare_pair(
        index, arrived, gains, prepared, rows, block_rows, first_part
    )

    place = ((z >> 1) if exchanging else jnp.zeros_like(z)).astype(jnp.int32).reshape(1)
    bias = qkv_bias.astype(F32)
    bias = choose(low, bias[:, :extent], bias[:, extent:])[0].reshape(1, -1)
    attention = exchange_attention if exchanging else gathered_attention
    send = (lambda item: swap(item, "ctx", 2)) if exchanging else (lambda item: item)
    packed, first_block = [], 0
    for begin, end in parts:
        ranks = jnp.transpose(ranks_of(order[begin:end], (0, 1))).reshape(-1)
        count = 2 * (end - begin)
        waits = [forward_column] if packed else []
        mine, other = project(
            place, ranks, one, g_both, first_block, count, table, bias, pieces, block_rows, waits
        )
        if not packed:
            forward_column[0], mine = lax.optimization_barrier((forward_column[0], mine))
            forward_column = jnp.concatenate(forward_column, axis=0)
            forward_pieces = gather_pieces(forward_column)
        packed.append((first_block * block_rows, mine, other))
        first_block += count

    two, one_t, two_t, g_t = prepare_late(index, x_both, g_both, one, gains, rows, block_rows, (packed[1][1],))
    up_shift = up_bias.astype(F32).reshape(2, 1, hidden)
    up_shift = choose(low, up_shift[0], up_shift[1])[0]
    arrivals = [send(theirs) for _, _, theirs in packed]
    returned = [attention(packed[0][1], arrivals[0], order[: parts[0][1]], table, block_rows, (g_t,))]
    branch, slope, up_sum, forward_grads = feed_forward(
        two, g_both, two_t, g_t, up_shift, forward_pieces, (returned[0][0],)
    )
    returned.append(attention(packed[1][1], arrivals[1], order[parts[1][0] :], table, block_rows, (up_sum,)))

    scalars = jnp.stack([f * ctx + z, place[0], low, core]).astype(jnp.int32)
    end_shift = (out_bias.astype(F32) + down_bias.astype(F32)).reshape(1, width)
    forward_terms = scatter(forward_grads)
    pairs = range(2, ctx, 2)

    def finish_part(number, small, waits):
        first, (local, remote) = packed[number][0], returned[number]
        mine, theirs, small = finish(
            scalars, x_both, gains, branch, slope, first, local, remote, small, pieces, rows, waits
        )
        return (mine, swap(theirs, "tp", 1)), small

    def weights_part(number, before, waits):
        first, (local, remote) = packed[number][0], returned[number]
        return attention_weights(place, one_t, g_t, first, local, remote, before, len(pieces), waits)

    zero = jnp.zeros((1, width), F32)
    small = jnp.concatenate([zero] * 4 + [grad_sum, zero, zero, *choose(low, up_sum, zero)] + [zero] * (SMALL_ROWS - 9))
    made = {}

    def run(task, wait):
        if task == "finish_a":
            made["a"], made["small"] = finish_part(0, small, (wait,))
            return made["small"]
        if task == "weights_a":
            made["grads_a"] = weights_part(0, None, (wait,))
            return made["grads_a"]
        if task == "forward_first":
            keep, *send = reduce_and_cut(
                forward_terms, [(0, 2 * rows, F32)] + [(j * rows, 2 * rows, BF16) for j in pairs], (wait,)
            )
            made["forward"] = [keep] + [swap(item, "ctx", j) for j, item in zip(pairs, send)]
            return keep
        if task == "finish_b":
            made["b"], made["small"] = finish_part(1, made["small"], (wait,))
            return made["small"]
        if task == "weights_b":
            grads = weights_part(1, (made["grads_a"], made["small"]), (wait,))
            made["attention"] = scatter(grads)
            return grads[0]
        if task == "forward_second":
            made["mine"], made["send"] = reduce_and_cut(
                made["forward"], [(0, rows, F32), (rows, rows, BF16)], (wait,)
            )
            return made["mine"]
        if task == "attention_first":
            made["keep"], *send = reduce_and_cut(
                made["attention"],
                [(0, rows, F32)] + [(j * rows, rows, BF16) for j in range(1, ctx)],
                (wait,),
                SMALL_ROWS,
            )
            made["sent"] = [swap(item, "ctx", j) for j, item in enumerate(send, 1)]
            return made["keep"]
        if task == "sums":
            sums = core_sums(1, [*made["a"], *made["b"]], (), (wait,))
            made["pair"] = swap(sums, "ctx", 1)
            return sums
        if task == "totals":
            totals = core_sums(0, [*made["a"], *made["b"]], [made["pair"]], (wait, *made["sent"]))
            made["totals"] = (totals, swap(totals, "tp", 1))
            return totals
        core_place = core.astype(jnp.int32).reshape(1)
        made["results"] = close(core_place, x, g, *made["totals"], end_shift, packed[1][0] // 2, (wait,))
        return made["results"][0]

    wait = returned[1][0]
    for task in TASKS:
        wait = run(task, wait)
    forward_mine, forward_send, attention_keep, results = (made[key] for key in ("mine", "send", "keep", "results"))
    attention_got = made["sent"]
    forward_got, done = lax.optimization_barrier((swap(forward_send, "ctx", 1), results[0]))
    results = [done, results[1]]
    outputs, input_grad = (item.reshape(inputs.shape) for item in results)
    forward_sums = choose(low, forward_mine, forward_got.astype(F32))
    up_sums = jnp.concatenate([half[0] for half in forward_sums], axis=1)
    down_sums = jnp.concatenate([jnp.transpose(half[1]) for half in forward_sums], axis=0)

    terms = [attention_keep[0]] + [got[0].astype(F32) for got in attention_got]
    halves = choose(low, tree_sum([term[:rows] for term in terms[::2]]), tree_sum([term[:rows] for term in terms[1::2]]))
    small = tree_sum([term[rows:] for term in terms])
    fields = [
        jnp.concatenate([half[:, i * extent : (i + 1) * extent] for half in halves], axis=1) for i in range(4)
    ]
    norm_sums = small[:4] + swap(small[:4], "tp", 1)
    pre_sums = small[5:7, : 3 * extent].reshape(2, 3, extent)
    return (
        outputs,
        input_grad,
        norm_sums[0],
        norm_sums[1],
        norm_sums[2],
        norm_sums[3],
        jnp.stack(fields[:3]),
        jnp.concatenate([pre_sums[0], pre_sums[1]], axis=1),
        jnp.transpose(fields[3]),
        small[4],
        up_sums,
        small[7:9].reshape(-1),
        down_sums,
        small[4],
    )


def solution(mesh):
    placed = (
        P(None, "ctx", "fsdp", None),
        P(None, "fsdp", None),
        P(),
        P(),
        P(),
        P(),
        P(None, ("fsdp", "ctx"), "tp"),
        P(None, "tp"),
        P("tp", ("fsdp", "ctx")),
        P(),
        P(("fsdp", "ctx"), "tp"),
        P("tp"),
        P("tp", ("fsdp", "ctx")),
        P(),
        P(None, "ctx", "fsdp", None),
    )
    return jax.shard_map(
        local,
        mesh=mesh,
        in_specs=placed,
        out_specs=(
            P(None, "ctx", "fsdp", None),
            P(None, "ctx", "fsdp", None),
            P(),
            P(),
            P(),
            P(),
            P(None, ("fsdp", "ctx"), "tp"),
            P(None, "tp"),
            P("tp", ("fsdp", "ctx")),
            P(),
            P(("fsdp", "ctx"), "tp"),
            P("tp"),
            P("tp", ("fsdp", "ctx")),
            P(),
        ),
        check_vma=False,
    )
```

profile of v0, /device:TPU:0, one launch (start us, length us, event | category | flops | bytes accessed | tf_op | source)
XLA Modules:
  0.0 344.6 jit_solution(4863820026650179490)
XLA Ops:
  6.6 3.0 collective-permute-start
  20.0 4.2 %collective-permute-done.2 = bf16[64,1024]{1,0:T(8,128)(2,1)} collective-permute-done((bf16[64,1024]{1,0:T(8,128)(2,1)}, bf16[64,1024]{1,0:T(8,128)(2,1)}, u32[]{:S(2)}, u32[]{:S(2)}) %collective-permute-start.2) | collective-permute-done | bytes 131104 | tf_op jit(solution)/shard_map/ppermute | solution.py:35
  30.0 3.6 %prepare_own.1 = (bf16[768,1024]{1,0:T(8,128)(2,1)S(1)}, bf16[768,1024]{1,0:T(8,128)(2,1)S(1)}, bf16[768,1024]{1,0:T(8,128)(2,1)S(1)}, f32[1,1024]{1,0:T(1,128)S(1)}) custom-call(s32[2]{0:T(128)S(1)} %pad_add_fusion.refs_0_, bf16[768,1024]{1,0:T(8,128)(2,1)S(1)} %bitcast.99, bf16[768,1024]{1,0:T(8,128)(2,1)S(1)} %bitcast.102, ...), custom_call_target="tpu_custom_call" | custom-call | flops 3849999872 | bytes 1024 | tf_op jit(solution)/shard_map/prepare_own/pallas_call | solution.py:56
  37.2 3.2 collective-permute-done.5.refs_6_.refs_9_
  40.3 10.5 %collective-permute-done.6.refs_7_.refs_10_ = bf16[256,1024]{1,0:T(8,128)(2,1)S(1)} collective-permute-done((bf16[256,1024]{1,0:T(8,128)(2,1)S(1)}, bf16[256,1024]{1,0:T(8,128)(2,1)S(1)}, u32[]{:S(2)}, u32[]{:S(2)}) %collective-permute-start.6) | collective-permute-done | bytes 524320 | tf_op jit(solution)/shard_map/ppermute | solution.py:35
  50.8 9.2 %collective-permute-done.1.refs_1_ = bf16[2,768,512]{2,1,0:T(8,128)(2,1)} collective-permute-done((bf16[2,768,512]{2,1,0:T(8,128)(2,1)}, bf16[2,768,512]{2,1,0:T(8,128)(2,1)}, u32[]{:S(2)}, u32[]{:S(2)}) %collective-permute-start.1) | collective-permute-done | bytes 1572896 | tf_op jit(solution)/shard_map/ppermute | solution.py:35
  68.0 5.3 %prepare_pair.1 = (bf16[1536,1024]{1,0:T(8,128)(2,1)S(1)}, bf16[1536,1024]{1,0:T(8,128)(2,1)S(1)}, bf16[1536,1024]{1,0:T(8,128)(2,1)S(1)}) custom-call(s32[2]{0:T(128)S(1)} %pad_add_fusion.refs_0_, bf16[2,768,512]{2,1,0:T(8,128)(2,1)} %collective-permute-done.1.refs_1_, bf16[2,768,512]{2,1,0:T(8,128)(2,1)} %collective-permute-done.8.refs_2_, ...), custom_call_target="tpu_custom_call" | custom-call | flops 3849999872 | bytes 1024 | tf_op jit(solution)/shard_map/prepare_pair/pallas_call | solution.py:56
  73.3 3.3 project.2
  77.8 32.5 %collective-permute-done.9 = bf16[128,2048]{1,0:T(8,128)(2,1)S(1)} collective-permute-done((bf16[128,2048]{1,0:T(8,128)(2,1)}, bf16[128,2048]{1,0:T(8,128)(2,1)S(1)}, u32[]{:S(2)}, u32[]{:S(2)}) %collective-permute-start.9) | collective-permute-done | bytes 524320 | tf_op jit(solution)/shard_map/ppermute | solution.py:35
  116.6 5.9 %prepare_late.1 = (bf16[1536,1024]{1,0:T(8,128)(2,1)S(1)}, bf16[1024,1536]{1,0:T(8,128)(2,1)S(1)}, bf16[1024,1536]{1,0:T(8,128)(2,1)S(1)}, bf16[1024,1536]{1,0:T(8,128)(2,1)S(1)}) custom-call(s32[2]{0:T(128)S(1)} %pad_add_fusion.refs_0_, bf16[1536,1024]{1,0:T(8,128)(2,1)S(1)} %get-tuple-element.85.refs_1_, ...), custom_call_target="tpu_custom_call" | custom-call | flops 6600000000 | bytes 1024 | tf_op jit(solution)/shard_map/prepare_late/pallas_call | solution.py:56
  124.1 19.9 %collective-permute-done.13 = bf16[1024,512]{1,0:T(8,128)(2,1)S(1)} collective-permute-done((bf16[1024,512]{1,0:T(8,128)(2,1)S(1)}, bf16[1024,512]{1,0:T(8,128)(2,1)S(1)}, u32[]{:S(2)}, u32[]{:S(2)}) %collective-permute-start.13) | collective-permute-done | bytes 1048608 | tf_op jit(solution)/shard_map/ppermute | solution.py:35
  144.0 18.2 %attend.2 = (bf16[2,2,256,512]{3,2,1,0:T(8,128)(2,1)S(1)}, bf16[2,2,256,512]{3,2,1,0:T(8,128)(2,1)}) custom-call(s32[8]{0:T(128)S(1)} %reshape.372.refs_0_, f32[2,1024,128]{2,1,0:T(8,128)S(1)} %pad_maximum_fusion.1.refs_6_.refs_3_.refs_1_, bf16[2,2,256,512]{3,2,1,0:T(8,128)(2,1)S(1)} %bitcast.113, bf16[2,2,256,512]{3,2,1,0:T(8,128)(2,1)S(1)} %bitcast.110, ...), custom_call_target="tpu_custom_call" | custom-call | flops 40333332480 | bytes 1024 | tf_op jit(solution)/shard_map/attend/pallas_call | solution.py:56
  165.2 31.4 %feed_forward.1 = (f32[1536,1024]{1,0:T(8,128)}, f32[1536,1024]{1,0:T(8,128)}, f32[1,1024]{1,0:T(1,128)}, f32[2,256,1024]{2,1,0:T(8,128)}, bf16[2,256,1024]{2,1,...) custom-call(bf16[1536,1024]{1,0:T(8,128)(2,1)} %copy-done.46, ...), custom_call_target="tpu_custom_call" | custom-call | flops 62333333504 | bytes 1024 | tf_op jit(solution)/shard_map/feed_forward/pallas_call | solution.py:56
  203.9 10.0 %attend.3 = (bf16[2,1,256,512]{3,2,1,0:T(8,128)(2,1)S(1)}, bf16[2,1,256,512]{3,2,1,0:T(8,128)(2,1)}) custom-call(s32[4]{0:T(128)S(1)} %select_reduce_fusion.1.refs_0_, f32[2,1024,128]{2,1,0:T(8,128)S(1)} %copy-done.3, bf16[2,1,256,512]{3,2,1,0:T(8,128)(2,1)S(1)} %bitcast.111, bf16[2,1,256,512]{3,2,1,0:T(8,128)(2,1)S(1)} %bitcast.112, f32[1,1024]{1,0:T(1,128)S(1)} %copy-done.29), custom_call_target="tpu_custom_call" | custom-call | flops 20166666240 | bytes 1024 | tf_op jit(solution)/shard_map/attend/pallas_call | solution.py:56
  222.8 12.8 %finish.2 = (bf16[2,2,256,1024]{3,2,1,0:T(8,128)(2,1)S(1)}, bf16[2,2,256,1024]{3,2,1,0:T(8,128)(2,1)}, f32[16,1024]{1,0:T(8,128)S(1)}) custom-call(s32[4]{0:T(128)S(1)} %pad_add_fusion.3.refs_0_, bf16[1536,1024]{1,0:T(8,128)(2,1)S(1)} %copy-done.5, f32[4,1024]{1,0:T(4,128)S(1)} %maximum_convert_fusion.refs_3_.refs_4_.refs_2_, ...), custom_call_target="tpu_custom_call" | custom-call | flops 916666688 | bytes 1024 | tf_op jit(solution)/shard_map/finish/pallas_call | solution.py:56
  236.9 3.8 %attention_weights.2.refs_4_.refs_5_ = f32[4,256,1024]{2,1,0:T(8,128)S(1)} custom-call(s32[1]{0:T(128)} %bitcast.19.refs_0_, bf16[1024,1536]{1,0:T(8,128)(2,1)S(1)} %copy-done.7, bf16[1024,1536]{1,0:T(8,128)(2,1)S(1)} %copy-done.9, bf16[1024,512]{1,0:T(8,128)(2,1)S(1)} %bitcast.97, bf16[1024,512]{1,0:T(8,128)(2,1)S(1)} %collective-permute-done.17.refs_6_.refs_4_, ...), custom_call_target="tpu_custom_call" | custom-call | flops 916666688 | bytes 1024 | tf_op jit(solution)/shard_map/attention_weights/pallas_call | solution.py:56
  240.8 5.0 %collective-permute-done.15.refs_2_ = bf16[2,256,1024]{2,1,0:T(8,128)(2,1)} collective-permute-done((bf16[2,256,1024]{2,1,0:T(8,128)(2,1)}, bf16[2,256,1024]{2,1,0:T(8,128)(2,1)}, u32[]{:S(2)}, u32[]{:S(2)}) %collective-permute-start.15) | collective-permute-done | bytes 1048608 | tf_op jit(solution)/shard_map/ppermute | solution.py:35
  245.7 3.0 reduce_and_cut.3
  248.8 7.6 %finish.3 = (bf16[2,2,128,1024]{3,2,1,0:T(8,128)(2,1)S(1)}, bf16[2,2,128,1024]{3,2,1,0:T(8,128)(2,1)S(1)}, f32[16,1024]{1,0:T(8,128)S(1)}) custom-call(s32[4]{0:T(128)S(1)} %pad_add_fusion.3.refs_0_, bf16[1536,1024]{1,0:T(8,128)(2,1)S(1)} %copy-done.5, f32[4,1024]{1,0:T(4,128)S(1)} %maximum_convert_fusion.refs_3_.refs_4_.refs_2_, ...), custom_call_target="tpu_custom_call" | custom-call | flops 11733332992 | bytes 1024 | tf_op jit(solution)/shard_map/finish/pallas_call | solution.py:56
  259.2 3.7 %attention_weights.3 = (f32[1,272,1024]{2,1,0:T(8,128)S(1)}, bf16[1,272,1024]{2,1,0:T(8,128)(2,1)S(1)}, bf16[1,272,1024]{2,1,0:T(8,128)(2,1)S(1)}, bf16[1,272,1024]{2,1,0:T(8,128)(2,1)S(1)}) custom-call(s32[1]{0:T(128)} %bitcast.19.refs_0_, bf16[1024,1536]{1,0:T(8,128)(2,1)S(1)} %copy-done.7, bf16[1024,1536]{1,0:T(8,128)(2,1)S(1)} %copy-done.9, ...), custom_call_target="tpu_custom_call" | custom-call | flops 12833333248 | bytes 1024 | tf_op jit(solution)/shard_map/attention_weights/pallas_call | solution.py:56
  269.3 13.8 %collective-permute-done.19.refs_1_ = bf16[2,128,1024]{2,1,0:T(8,128)(2,1)S(1)} collective-permute-done((bf16[2,128,1024]{2,1,0:T(8,128)(2,1)S(1)}, bf16[2,128,1024]{2,1,0:T(8,128)(2,1)S(1)}, u32[]{:S(2)}, u32[]{:S(2)}) %collective-permute-start.19) | collective-permute-done | bytes 524320 | tf_op jit(solution)/shard_map/ppermute | solution.py:35
  284.5 4.4 %collective-permute-done.26.refs_2_ = bf16[1,272,1024]{2,1,0:T(8,128)(2,1)S(1)} collective-permute-done((bf16[1,272,1024]{2,1,0:T(8,128)(2,1)S(1)}, bf16[1,272,1024]{2,1,0:T(8,128)(2,1)S(1)}, u32[]{:S(2)}, u32[]{:S(2)}) %collective-permute-start.26) | collective-permute-done | bytes 557088 | tf_op jit(solution)/shard_map/ppermute | solution.py:35
  295.7 30.2 %collective-permute-done.28.refs_6_ = bf16[1,80,1024]{2,1,0:T(8,128)(2,1)S(1)} collective-permute-done((bf16[1,80,1024]{2,1,0:T(8,128)(2,1)S(1)}, bf16[1,80,1024]{2,1,0:T(8,128)(2,1)S(1)}, u32[]{:S(2)}, u32[]{:S(2)}) %collective-permute-start.28) | collective-permute-done | bytes 163872 | tf_op jit(solution)/shard_map/ppermute | solution.py:35
  336.7 4.3 %close.1 = (bf16[768,1024]{1,0:T(8,128)(2,1)}, bf16[768,1024]{1,0:T(8,128)(2,1)}) custom-call(s32[1]{0:T(128)} %bitcast.1.refs_0_, bf16[768,1024]{1,0:T(8,128)(2,1)S(1)} %bitcast.100, bf16[768,1024]{1,0:T(8,128)(2,1)S(1)} %bitcast.103, bf16[2,384,1024]{2,1,0:T(8,128)(2,1)S(1)} %core_sums.3.refs_3_.refs_6_, ...), custom_call_target="tpu_custom_call" | custom-call | flops 5500000256 | bytes 1024 | tf_op jit(solution)/shard_map/close/pallas_call | solution.py:56
  (273 shorter events, 94.2 us)
Async XLA Ops:
  17.1 42.9 %collective-permute-start.1 = (bf16[2,768,512]{2,1,0:T(8,128)(2,1)}, bf16[2,768,512]{2,1,0:T(8,128)(2,1)}, u32[]{:S(2)}, u32[]{:S(2)}) collective-permute-start(bf16[2,768,512]{2,1,0:T(8,128)(2,1)} %slice_select_fusion), channel_id=1, source_target_pairs={{0,2},{2,0},{4,6},{6,4},{1,3},{3,1},{5,7},{7,5},{8,10},{10,8},{12,... | collective-permute-start | bytes 4718600 | tf_op jit(solution)/shard_map/ppermute | solution.py:35
  27.0 23.9 %collective-permute-start.6 = (bf16[256,1024]{1,0:T(8,128)(2,1)S(1)}, bf16[256,1024]{1,0:T(8,128)(2,1)S(1)}, u32[]{:S(2)}, u32[]{:S(2)}) collective-permute-start(bf16[256,1024]{1,0:T(8,128)(2,1)S(1)} %pad_maximum_fusion.3.refs_4_.refs_5_.refs_8_), channel_id=1, source_target_pairs={{0,16},{8,24},{16,0},{24,8},{1,17},{9,25},{17,1},{25,9},{2,18},{10... | collective-permute-start | bytes 1572872 | tf_op jit(solution)/shard_map/ppermute | solution.py:35
  28.5 22.3 %collective-permute-start.7 = (bf16[256,1024]{1,0:T(8,128)(2,1)S(1)}, bf16[256,1024]{1,0:T(8,128)(2,1)S(1)}, u32[]{:S(2)}, u32[]{:S(2)}) collective-permute-start(bf16[256,1024]{1,0:T(8,128)(2,1)S(1)} %pad_maximum_fusion.3.refs_4_.refs_5_.refs_8_), channel_id=1, source_target_pairs={{0,24},{8,16},{16,8},{24,0},{1,25},{9,17},{17,9},{25,1},{2,26},{10... | collective-permute-start | bytes 1572872 | tf_op jit(solution)/shard_map/ppermute | solution.py:35
  61.5 48.8 %collective-permute-start.9 = (bf16[128,2048]{1,0:T(8,128)(2,1)}, bf16[128,2048]{1,0:T(8,128)(2,1)S(1)}, u32[]{:S(2)}, u32[]{:S(2)}) collective-permute-start(bf16[128,2048]{1,0:T(8,128)(2,1)} %copy-done.18), channel_id=1, source_target_pairs={{0,4},{2,6},{4,0},{6,2},{1,5},{3,7},{5,1},{7,3},{8,12},{10,14},{12... | collective-permute-start | bytes 1572872 | tf_op jit(solution)/shard_map/ppermute | solution.py:35
  76.6 67.5 %collective-permute-start.13 = (bf16[1024,512]{1,0:T(8,128)(2,1)S(1)}, bf16[1024,512]{1,0:T(8,128)(2,1)S(1)}, u32[]{:S(2)}, u32[]{:S(2)}) collective-permute-start(bf16[1024,512]{1,0:T(8,128)(2,1)S(1)} %get-tuple-element.99), channel_id=1, source_target_pairs={{0,4},{2,6},{4,0},{6,2},{1,5},{3,7},{5,1},{7,3},{8,12},{10,14},{12... | collective-permute-start | bytes 3145736 | tf_op jit(solution)/shard_map/ppermute | solution.py:35
  110.4 52.9 %collective-permute-start.10 = (bf16[256,2048]{1,0:T(8,128)(2,1)S(1)}, bf16[256,2048]{1,0:T(8,128)(2,1)S(1)}, u32[]{:S(2)}, u32[]{:S(2)}) collective-permute-start(bf16[256,2048]{1,0:T(8,128)(2,1)S(1)} %constant_dynamic-update-slice_fusion.refs_9_.refs_5_), channel_id=1, source_target_pairs={{0,8},{8,0},{16,24},{24,16},{1,9},{9,1},{17,25},{25,17},{2,10},{10... | collective-permute-start | bytes 3145736 | tf_op jit(solution)/shard_map/ppermute | solution.py:35
  111.9 51.3 %collective-permute-start.11 = (bf16[256,2048]{1,0:T(8,128)(2,1)S(1)}, bf16[256,2048]{1,0:T(8,128)(2,1)S(1)}, u32[]{:S(2)}, u32[]{:S(2)}) collective-permute-start(bf16[256,2048]{1,0:T(8,128)(2,1)S(1)} %constant_dynamic-update-slice_fusion.refs_9_.refs_5_), channel_id=1, source_target_pairs={{0,16},{8,24},{16,0},{24,8},{1,17},{9,25},{17,1},{25,9},{2,18},{10... | collective-permute-start | bytes 3145736 | tf_op jit(solution)/shard_map/ppermute | solution.py:35
  113.4 49.8 %collective-permute-start.12 = (bf16[256,2048]{1,0:T(8,128)(2,1)S(1)}, bf16[256,2048]{1,0:T(8,128)(2,1)S(1)}, u32[]{:S(2)}, u32[]{:S(2)}) collective-permute-start(bf16[256,2048]{1,0:T(8,128)(2,1)S(1)} %constant_dynamic-update-slice_fusion.refs_9_.refs_5_), channel_id=1, source_target_pairs={{0,24},{8,16},{16,8},{24,0},{1,25},{9,17},{17,9},{25,1},{2,26},{10... | collective-permute-start | bytes 3145736 | tf_op jit(solution)/shard_map/ppermute | solution.py:35
  116.5 83.6 %collective-permute-start.18 = (bf16[512,512]{1,0:T(8,128)(2,1)}, bf16[512,512]{1,0:T(8,128)(2,1)S(1)}, u32[]{:S(2)}, u32[]{:S(2)}) collective-permute-start(bf16[512,512]{1,0:T(8,128)(2,1)} %get-tuple-element.111), channel_id=1, source_target_pairs={{0,4},{2,6},{4,0},{6,2},{1,5},{3,7},{5,1},{7,3},{8,12},{10,14},{12... | collective-permute-start | bytes 1572872 | tf_op jit(solution)/shard_map/ppermute | solution.py:35
  163.2 54.5 %collective-permute-start.17 = (bf16[1024,512]{1,0:T(8,128)(2,1)}, bf16[1024,512]{1,0:T(8,128)(2,1)S(1)}, u32[]{:S(2)}, u32[]{:S(2)}) collective-permute-start(bf16[1024,512]{1,0:T(8,128)(2,1)} %bitcast.27), channel_id=1, source_target_pairs={{0,4},{2,6},{4,0},{6,2},{1,5},{3,7},{5,1},{7,3},{8,12},{10,14},{12... | collective-permute-start | bytes 3145736 | tf_op jit(solution)/shard_map/ppermute | solution.py:35
  196.6 44.2 %collective-permute-start.14 = (bf16[2,256,1024]{2,1,0:T(8,128)(2,1)}, bf16[2,256,1024]{2,1,0:T(8,128)(2,1)}, u32[]{:S(2)}, u32[]{:S(2)}) collective-permute-start(bf16[2,256,1024]{2,1,0:T(8,128)(2,1)} %get-tuple-element.102), channel_id=1, source_target_pairs={{0,8},{8,0},{16,24},{24,16},{1,9},{9,1},{17,25},{25,17},{2,10},{10... | collective-permute-start | bytes 3145736 | tf_op jit(solution)/shard_map/ppermute | solution.py:35
  198.1 47.6 %collective-permute-start.15 = (bf16[2,256,1024]{2,1,0:T(8,128)(2,1)}, bf16[2,256,1024]{2,1,0:T(8,128)(2,1)}, u32[]{:S(2)}, u32[]{:S(2)}) collective-permute-start(bf16[2,256,1024]{2,1,0:T(8,128)(2,1)} %get-tuple-element.103), channel_id=1, source_target_pairs={{0,16},{8,24},{16,0},{24,8},{1,17},{9,25},{17,1},{25,9},{2,18},{10... | collective-permute-start | bytes 3145736 | tf_op jit(solution)/shard_map/ppermute | solution.py:35
  199.7 46.1 %collective-permute-start.16 = (bf16[2,256,1024]{2,1,0:T(8,128)(2,1)}, bf16[2,256,1024]{2,1,0:T(8,128)(2,1)}, u32[]{:S(2)}, u32[]{:S(2)}) collective-permute-start(bf16[2,256,1024]{2,1,0:T(8,128)(2,1)} %get-tuple-element.104), channel_id=1, source_target_pairs={{0,24},{8,16},{16,8},{24,0},{1,25},{9,17},{17,9},{25,1},{2,26},{10... | collective-permute-start | bytes 3145736 | tf_op jit(solution)/shard_map/ppermute | solution.py:35
  214.7 34.1 %collective-permute-start.21 = (bf16[512,512]{1,0:T(8,128)(2,1)}, bf16[512,512]{1,0:T(8,128)(2,1)}, u32[]{:S(2)}, u32[]{:S(2)}) collective-permute-start(bf16[512,512]{1,0:T(8,128)(2,1)} %bitcast.32), channel_id=1, source_target_pairs={{0,4},{2,6},{4,0},{6,2},{1,5},{3,7},{5,1},{7,3},{8,12},{10,14},{12... | collective-permute-start | bytes 1572872 | tf_op jit(solution)/shard_map/ppermute | solution.py:35
  236.9 29.6 %collective-permute-start.20 = (bf16[2,2,256,1024]{3,2,1,0:T(8,128)(2,1)}, bf16[2,2,256,1024]{3,2,1,0:T(8,128)(2,1)}, u32[]{:S(2)}, u32[]{:S(2)}) collective-permute-start(bf16[2,2,256,1024]{3,2,1,0:T(8,128)(2,1)} %get-tuple-element.117), channel_id=1, source_target_pairs={{0,1},{1,0},{2,3},{3,2},{4,5},{5,4},{6,7},{7,6},{8,9},{9,8},{10,11... | collective-permute-start | bytes 6291464 | tf_op jit(solution)/shard_map/ppermute | solution.py:35
  256.5 26.6 %collective-permute-start.19 = (bf16[2,128,1024]{2,1,0:T(8,128)(2,1)S(1)}, bf16[2,128,1024]{2,1,0:T(8,128)(2,1)S(1)}, u32[]{:S(2)}, u32[]{:S(2)}) collective-permute-start(bf16[2,128,1024]{2,1,0:T(8,128)(2,1)S(1)} %get-tuple-element.115), channel_id=1, source_target_pairs={{0,4},{2,6},{4,0},{6,2},{1,5},{3,7},{5,1},{7,3},{8,12},{10,14},{12... | collective-permute-start | bytes 1572872 | tf_op jit(solution)/shard_map/ppermute | solution.py:35
  262.9 21.6 %collective-permute-start.25 = (bf16[1,272,1024]{2,1,0:T(8,128)(2,1)S(1)}, bf16[1,272,1024]{2,1,0:T(8,128)(2,1)S(1)}, u32[]{:S(2)}, u32[]{:S(2)}) collective-permute-start(bf16[1,272,1024]{2,1,0:T(8,128)(2,1)S(1)} %get-tuple-element.124), channel_id=1, source_target_pairs={{0,8},{8,0},{16,24},{24,16},{1,9},{9,1},{17,25},{25,17},{2,10},{10... | collective-permute-start | bytes 1671176 | tf_op jit(solution)/shard_map/ppermute | solution.py:35
  264.2 24.7 %collective-permute-start.26 = (bf16[1,272,1024]{2,1,0:T(8,128)(2,1)S(1)}, bf16[1,272,1024]{2,1,0:T(8,128)(2,1)S(1)}, u32[]{:S(2)}, u32[]{:S(2)}) collective-permute-start(bf16[1,272,1024]{2,1,0:T(8,128)(2,1)S(1)} %get-tuple-element.125), channel_id=1, source_target_pairs={{0,16},{8,24},{16,0},{24,8},{1,17},{9,25},{17,1},{25,9},{2,18},{10... | collective-permute-start | bytes 1671176 | tf_op jit(solution)/shard_map/ppermute | solution.py:35
  265.1 25.5 %collective-permute-start.27 = (bf16[1,272,1024]{2,1,0:T(8,128)(2,1)S(1)}, bf16[1,272,1024]{2,1,0:T(8,128)(2,1)S(1)}, u32[]{:S(2)}, u32[]{:S(2)}) collective-permute-start(bf16[1,272,1024]{2,1,0:T(8,128)(2,1)S(1)} %get-tuple-element.126), channel_id=1, source_target_pairs={{0,24},{8,16},{16,8},{24,0},{1,25},{9,17},{17,9},{25,1},{2,26},{10... | collective-permute-start | bytes 1671176 | tf_op jit(solution)/shard_map/ppermute | solution.py:35
  268.9 59.3 %collective-permute-start.24 = (bf16[2,384,1024]{2,1,0:T(8,128)(2,1)}, bf16[2,384,1024]{2,1,0:T(8,128)(2,1)}, u32[]{:S(2)}, u32[]{:S(2)}) collective-permute-start(bf16[2,384,1024]{2,1,0:T(8,128)(2,1)} %core_sums.2.refs_2_), channel_id=1, source_target_pairs={{0,2},{2,0},{4,6},{6,4},{1,3},{3,1},{5,7},{7,5},{8,10},{10,8},{12,... | collective-permute-start | bytes 4718600 | tf_op jit(solution)/shard_map/ppermute | solution.py:35
  291.2 34.7 %collective-permute-start.28 = (bf16[1,80,1024]{2,1,0:T(8,128)(2,1)S(1)}, bf16[1,80,1024]{2,1,0:T(8,128)(2,1)S(1)}, u32[]{:S(2)}, u32[]{:S(2)}) collective-permute-start(bf16[1,80,1024]{2,1,0:T(8,128)(2,1)S(1)} %get-tuple-element.129), channel_id=1, source_target_pairs={{0,2},{2,0},{4,6},{6,4},{1,3},{3,1},{5,7},{7,5},{8,10},{10,8},{12,... | collective-permute-start | bytes 491528 | tf_op jit(solution)/shard_map/ppermute | solution.py:35
  291.6 34.3 %collective-permute-start.29 = (bf16[1,80,1024]{2,1,0:T(8,128)(2,1)S(1)}, bf16[1,80,1024]{2,1,0:T(8,128)(2,1)S(1)}, u32[]{:S(2)}, u32[]{:S(2)}) collective-permute-start(bf16[1,80,1024]{2,1,0:T(8,128)(2,1)S(1)} %get-tuple-element.130), channel_id=1, source_target_pairs={{0,4},{2,6},{4,0},{6,2},{1,5},{3,7},{5,1},{7,3},{8,12},{10,14},{12... | collective-permute-start | bytes 491528 | tf_op jit(solution)/shard_map/ppermute | solution.py:35
  294.3 31.7 %collective-permute-start.30 = (bf16[1,80,1024]{2,1,0:T(8,128)(2,1)S(1)}, bf16[1,80,1024]{2,1,0:T(8,128)(2,1)S(1)}, u32[]{:S(2)}, u32[]{:S(2)}) collective-permute-start(bf16[1,80,1024]{2,1,0:T(8,128)(2,1)S(1)} %get-tuple-element.131), channel_id=1, source_target_pairs={{0,6},{2,4},{4,2},{6,0},{1,7},{3,5},{5,3},{7,1},{8,14},{10,12},{12... | collective-permute-start | bytes 491528 | tf_op jit(solution)/shard_map/ppermute | solution.py:35
  295.6 45.4 %collective-permute-start.23 = (bf16[2,64,1024]{2,1,0:T(8,128)(2,1)}, bf16[2,64,1024]{2,1,0:T(8,128)(2,1)}, u32[]{:S(2)}, u32[]{:S(2)}) collective-permute-start(bf16[2,64,1024]{2,1,0:T(8,128)(2,1)} %get-tuple-element.123), channel_id=1, source_target_pairs={{0,2},{2,0},{4,6},{6,4},{1,3},{3,1},{5,7},{7,5},{8,10},{10,8},{12,... | collective-permute-start | bytes 786440 | tf_op jit(solution)/shard_map/ppermute | solution.py:35
  (74 other events, 766.9 us)
where the time goes:
time: 349 us; the launch traced here: 345 us
  waiting for transfers between devices  135 us (39%)
  Pallas kernels  122 us (35%)
  starting transfers between devices  35.5 us (10%)
  local copies, waits for them, and re-layouts  32.8 us (9%)
  other arithmetic  17 us (5%)
    ppermute x33, waiting for transfers between devices, swap(): return lax.ppermute(value, axis, [(i, i ^ bit) for i in range(size)])  135 us
    pallas_call x18, Pallas kernels, launch(): pl.pallas_call(body, out_shape=out_shape, grid_spec=pltpu.PrefetchScalarG...  122 us
    ppermute x33, starting transfers between devices, swap(): return lax.ppermute(value, axis, [(i, i ^ bit) for i in range(size)])  35.5 us
    unnamed x135, local copies, waits for them, and re-layouts  28.8 us
  transfers between devices with their start and end apart: 33, of which 12 were waited for; matrix products, arithmetic and copies ran while one was open for 4% of the time, Pallas kernels for 35%

commit v1 on v0

--- a/solution.py
+++ b/solution.py
@@ -581,7 +581,7 @@
             pltpu.VMEM((8, width), F32),
         ],
         name="finish",
-        mib=40,
+        mib=60 if first == 0 else 40,
     )
 
 

time: 349 us -> 347 us (level)
    ppermute x33, waiting for transfers between devices: 135 us -> 132 us  [swap(): return lax.ppermute(value, axis, [(i, i ^ bit) for i in range(size)])]
    unnamed x135 -> x145, local copies, waits for them, and re-layouts: 28.8 us -> 26.1 us
  transfers between devices with their start and end apart: 33 -> 33, of which waited for: 12 -> 12; matrix products, arithmetic and copies ran while one was open for 4% -> 5% of each run, Pallas kernels for 35% -> 36%
where the time goes in v1:
time: 347 us; the launch traced here: 343 us
  waiting for transfers between devices  132 us (38%)
  Pallas kernels  125 us (36%)
  starting transfers between devices  35.2 us (10%)
  local copies, waits for them, and re-layouts  31.2 us (9%)
  other arithmetic  17.6 us (5%)
    ppermute x33, waiting for transfers between devices, swap(): return lax.ppermute(value, axis, [(i, i ^ bit) for i in range(size)])  132 us
    pallas_call x18, Pallas kernels, launch(): pl.pallas_call(body, out_shape=out_shape, grid_spec=pltpu.PrefetchScalarG...  125 us
    ppermute x33, starting transfers between devices, swap(): return lax.ppermute(value, axis, [(i, i ^ bit) for i in range(size)])  35.2 us
    unnamed x145, local copies, waits for them, and re-layouts  26.1 us
  transfers between devices with their start and end apart: 33, of which 12 were waited for; matrix products, arithmetic and copies ran while one was open for 5% of the time, Pallas kernels for 36%

profile of v1, /device:TPU:0, one launch (start us, length us, event | category | flops | bytes accessed | tf_op | source)
XLA Modules:
  0.0 343.0 jit_solution(8242426204949418778)
XLA Ops:
  6.6 3.0 collective-permute-start
  20.0 4.2 %collective-permute-done.2 = bf16[64,1024]{1,0:T(8,128)(2,1)} collective-permute-done((bf16[64,1024]{1,0:T(8,128)(2,1)}, bf16[64,1024]{1,0:T(8,128)(2,1)}, u32[]{:S(2)}, u32[]{:S(2)}) %collective-permute-start.2) | collective-permute-done | bytes 131104 | tf_op jit(solution)/shard_map/ppermute | solution.py:35
  30.0 4.0 %prepare_own.1 = (bf16[768,1024]{1,0:T(8,128)(2,1)S(1)}, bf16[768,1024]{1,0:T(8,128)(2,1)S(1)}, bf16[768,1024]{1,0:T(8,128)(2,1)S(1)}, f32[1,1024]{1,0:T(1,128)S(1)}) custom-call(s32[2]{0:T(128)S(1)} %pad_add_fusion.refs_0_, bf16[768,1024]{1,0:T(8,128)(2,1)S(1)} %bitcast.99, bf16[768,1024]{1,0:T(8,128)(2,1)S(1)} %bitcast.102, ...), custom_call_target="tpu_custom_call" | custom-call | flops 3849999872 | bytes 1024 | tf_op jit(solution)/shard_map/prepare_own/pallas_call | solution.py:56
  37.5 2.8 collective-permute-done.5.refs_6_.refs_9_
  40.4 10.5 %collective-permute-done.6.refs_7_.refs_10_ = bf16[256,1024]{1,0:T(8,128)(2,1)S(1)} collective-permute-done((bf16[256,1024]{1,0:T(8,128)(2,1)S(1)}, bf16[256,1024]{1,0:T(8,128)(2,1)S(1)}, u32[]{:S(2)}, u32[]{:S(2)}) %collective-permute-start.6) | collective-permute-done | bytes 524320 | tf_op jit(solution)/shard_map/ppermute | solution.py:35
  51.7 8.3 %collective-permute-done.1.refs_1_ = bf16[2,768,512]{2,1,0:T(8,128)(2,1)} collective-permute-done((bf16[2,768,512]{2,1,0:T(8,128)(2,1)}, bf16[2,768,512]{2,1,0:T(8,128)(2,1)}, u32[]{:S(2)}, u32[]{:S(2)}) %collective-permute-start.1) | collective-permute-done | bytes 1572896 | tf_op jit(solution)/shard_map/ppermute | solution.py:35
  68.0 5.3 %prepare_pair.1 = (bf16[1536,1024]{1,0:T(8,128)(2,1)S(1)}, bf16[1536,1024]{1,0:T(8,128)(2,1)S(1)}, bf16[1536,1024]{1,0:T(8,128)(2,1)S(1)}) custom-call(s32[2]{0:T(128)S(1)} %pad_add_fusion.refs_0_, bf16[2,768,512]{2,1,0:T(8,128)(2,1)} %collective-permute-done.1.refs_1_, bf16[2,768,512]{2,1,0:T(8,128)(2,1)} %collective-permute-done.8.refs_2_, ...), custom_call_target="tpu_custom_call" | custom-call | flops 3849999872 | bytes 1024 | tf_op jit(solution)/shard_map/prepare_pair/pallas_call | solution.py:56
  73.3 3.2 project.2
  77.9 32.7 %collective-permute-done.9 = bf16[128,2048]{1,0:T(8,128)(2,1)S(1)} collective-permute-done((bf16[128,2048]{1,0:T(8,128)(2,1)S(1)}, bf16[128,2048]{1,0:T(8,128)(2,1)S(1)}, u32[]{:S(2)}, u32[]{:S(2)}) %collective-permute-start.9) | collective-permute-done | bytes 524320 | tf_op jit(solution)/shard_map/ppermute | solution.py:35
  116.9 5.9 %prepare_late.1 = (bf16[1536,1024]{1,0:T(8,128)(2,1)S(1)}, bf16[1024,1536]{1,0:T(8,128)(2,1)S(1)}, bf16[1024,1536]{1,0:T(8,128)(2,1)S(1)}, bf16[1024,1536]{1,0:T(8,128)(2,1)S(1)}) custom-call(s32[2]{0:T(128)S(1)} %pad_add_fusion.refs_0_, bf16[1536,1024]{1,0:T(8,128)(2,1)S(1)} %get-tuple-element.85.refs_1_, ...), custom_call_target="tpu_custom_call" | custom-call | flops 6600000000 | bytes 1024 | tf_op jit(solution)/shard_map/prepare_late/pallas_call | solution.py:56
  124.4 19.9 %collective-permute-done.13 = bf16[1024,512]{1,0:T(8,128)(2,1)S(1)} collective-permute-done((bf16[1024,512]{1,0:T(8,128)(2,1)S(1)}, bf16[1024,512]{1,0:T(8,128)(2,1)S(1)}, u32[]{:S(2)}, u32[]{:S(2)}) %collective-permute-start.13) | collective-permute-done | bytes 1048608 | tf_op jit(solution)/shard_map/ppermute | solution.py:35
  144.3 17.5 %attend.2 = (bf16[2,2,256,512]{3,2,1,0:T(8,128)(2,1)S(1)}, bf16[2,2,256,512]{3,2,1,0:T(8,128)(2,1)S(1)}) custom-call(s32[8]{0:T(128)S(1)} %reshape.372.refs_0_, f32[2,1024,128]{2,1,0:T(8,128)S(1)} %pad_maximum_fusion.1.refs_6_.refs_3_.refs_1_, bf16[2,2,256,512]{3,2,1,0:T(8,128)(2,1)S(1)} %bitcast.113, bf16[2,2,256,512]{3,2,1,0:T(8,128)(2,1)S(1)} %bitcast.111, ...), custom_call_target="tpu_custom_call" | custom-call | flops 40333332480 | bytes 1024 | tf_op jit(solution)/shard_map/attend/pallas_call | solution.py:56
  164.7 31.4 %feed_forward.1 = (f32[1536,1024]{1,0:T(8,128)}, f32[1536,1024]{1,0:T(8,128)}, f32[1,1024]{1,0:T(1,128)}, f32[2,256,1024]{2,1,0:T(8,128)}, bf16[2,256,1024]{2,1,...) custom-call(bf16[1536,1024]{1,0:T(8,128)(2,1)} %copy-done.51, ...), custom_call_target="tpu_custom_call" | custom-call | flops 62333333504 | bytes 1024 | tf_op jit(solution)/shard_map/feed_forward/pallas_call | solution.py:56
  200.3 10.9 %attend.3 = (bf16[2,1,256,512]{3,2,1,0:T(8,128)(2,1)S(1)}, bf16[2,1,256,512]{3,2,1,0:T(8,128)(2,1)}) custom-call(s32[4]{0:T(128)S(1)} %select_reduce_fusion.1.refs_0_, f32[2,1024,128]{2,1,0:T(8,128)S(1)} %pad_maximum_fusion.1.refs_6_.refs_3_.refs_1_, bf16[2,1,256,512]{3,2,1,0:T(8,128)(2,1)S(1)} %bitcast.112, bf16[2,1,256,512]{3,2,1,0:T(8,128)(2,1)} %bitcast.30.refs_3_, ...), custom_call_target="tpu_custom_call" | custom-call | flops 20166666240 | bytes 1024 | tf_op jit(solution)/shard_map/attend/pallas_call | solution.py:56
  212.1 2.9 collective-permute-start.21
  217.3 15.4 %finish.2 = (bf16[2,2,256,1024]{3,2,1,0:T(8,128)(2,1)}, bf16[2,2,256,1024]{3,2,1,0:T(8,128)(2,1)}, f32[16,1024]{1,0:T(8,128)}) custom-call(s32[4]{0:T(128)} %pad_add_fusion.3.refs_0_, bf16[1536,1024]{1,0:T(8,128)(2,1)} %copy-done.6, f32[4,1024]{1,0:T(4,128)} %copy-done.33, f32[1536,1024]{1,0:T(8,128)} %get-tuple-element.107.refs_3_, ...), custom_call_target="tpu_custom_call" | custom-call | flops 916666688 | bytes 1024 | tf_op jit(solution)/shard_map/finish/pallas_call | solution.py:56
  238.6 3.8 %attention_weights.2.refs_4_.refs_5_ = f32[4,256,1024]{2,1,0:T(8,128)S(1)} custom-call(s32[1]{0:T(128)} %bitcast.19.refs_0_, bf16[1024,1536]{1,0:T(8,128)(2,1)S(1)} %copy-done.9, bf16[1024,1536]{1,0:T(8,128)(2,1)S(1)} %copy-done.12, bf16[1024,512]{1,0:T(8,128)(2,1)S(1)} %bitcast.97, bf16[1024,512]{1,0:T(8,128)(2,1)S(1)} %copy-done.5, f32[16,1024]{1,0:T(8,128)S(1)} %copy-done.31), custom_call_target="tpu_custom_call" | custom-call | flops 916666688 | bytes 1024 | tf_op jit(solution)/shard_map/attention_weights/pallas_call | solution.py:56
  242.5 2.8 collective-permute-done.15.refs_2_
  245.3 3.6 %reduce_and_cut.3 = (f32[2,128,1024]{2,1,0:T(8,128)S(1)}, bf16[2,128,1024]{2,1,0:T(8,128)(2,1)S(1)}) custom-call(f32[2,256,1024]{2,1,0:T(8,128)S(1)} %copy-done.50, bf16[2,256,1024]{2,1,0:T(8,128)(2,1)} %collective-permute-done.14.refs_1_, bf16[2,256,1024]{2,1,0:T(8,128)(2,1)} %collective-permute-done.15.refs_2_, ...), custom_call_target="tpu_custom_call" | custom-call | flops 5500000256 | bytes 1024 | tf_op jit(solution)/shard_map/reduce_and_cut/pallas_call | solution.py:56
  249.1 8.0 %finish.3 = (bf16[2,2,128,1024]{3,2,1,0:T(8,128)(2,1)S(1)}, bf16[2,2,128,1024]{3,2,1,0:T(8,128)(2,1)S(1)}, f32[16,1024]{1,0:T(8,128)S(1)}) custom-call(s32[4]{0:T(128)S(1)} %copy-done.36, bf16[1536,1024]{1,0:T(8,128)(2,1)S(1)} %copy-done.7, f32[4,1024]{1,0:T(4,128)S(1)} %copy-done.34, f32[1536,1024]{1,0:T(8,128)} %get-tuple-element.107.refs_3_, ...), custom_call_target="tpu_custom_call" | custom-call | flops 11733332992 | bytes 1024 | tf_op jit(solution)/shard_map/finish/pallas_call | solution.py:56
  269.9 13.9 %collective-permute-done.19.refs_1_ = bf16[2,128,1024]{2,1,0:T(8,128)(2,1)S(1)} collective-permute-done((bf16[2,128,1024]{2,1,0:T(8,128)(2,1)S(1)}, bf16[2,128,1024]{2,1,0:T(8,128)(2,1)S(1)}, u32[]{:S(2)}, u32[]{:S(2)}) %collective-permute-start.19) | collective-permute-done | bytes 524320 | tf_op jit(solution)/shard_map/ppermute | solution.py:35
  285.3 4.3 %collective-permute-done.26.refs_2_ = bf16[1,272,1024]{2,1,0:T(8,128)(2,1)S(1)} collective-permute-done((bf16[1,272,1024]{2,1,0:T(8,128)(2,1)S(1)}, bf16[1,272,1024]{2,1,0:T(8,128)(2,1)S(1)}, u32[]{:S(2)}, u32[]{:S(2)}) %collective-permute-start.26) | collective-permute-done | bytes 557088 | tf_op jit(solution)/shard_map/ppermute | solution.py:35
  296.3 30.2 %collective-permute-done.28.refs_6_ = bf16[1,80,1024]{2,1,0:T(8,128)(2,1)S(1)} collective-permute-done((bf16[1,80,1024]{2,1,0:T(8,128)(2,1)S(1)}, bf16[1,80,1024]{2,1,0:T(8,128)(2,1)S(1)}, u32[]{:S(2)}, u32[]{:S(2)}) %collective-permute-start.28) | collective-permute-done | bytes 163872 | tf_op jit(solution)/shard_map/ppermute | solution.py:35
  335.0 4.3 %close.1 = (bf16[768,1024]{1,0:T(8,128)(2,1)}, bf16[768,1024]{1,0:T(8,128)(2,1)}) custom-call(s32[1]{0:T(128)} %bitcast.1.refs_0_, bf16[768,1024]{1,0:T(8,128)(2,1)S(1)} %bitcast.100, bf16[768,1024]{1,0:T(8,128)(2,1)S(1)} %bitcast.103, bf16[2,384,1024]{2,1,0:T(8,128)(2,1)S(1)} %core_sums.3.refs_3_.refs_6_, ...), custom_call_target="tpu_custom_call" | custom-call | flops 5500000256 | bytes 1024 | tf_op jit(solution)/shard_map/close/pallas_call | solution.py:56
  (283 shorter events, 92.1 us)
Async XLA Ops:
  17.1 42.9 %collective-permute-start.1 = (bf16[2,768,512]{2,1,0:T(8,128)(2,1)}, bf16[2,768,512]{2,1,0:T(8,128)(2,1)}, u32[]{:S(2)}, u32[]{:S(2)}) collective-permute-start(bf16[2,768,512]{2,1,0:T(8,128)(2,1)} %slice_select_fusion), channel_id=1, source_target_pairs={{0,2},{2,0},{4,6},{6,4},{1,3},{3,1},{5,7},{7,5},{8,10},{10,8},{12,... | collective-permute-start | bytes 4718600 | tf_op jit(solution)/shard_map/ppermute | solution.py:35
  27.0 23.9 %collective-permute-start.6 = (bf16[256,1024]{1,0:T(8,128)(2,1)S(1)}, bf16[256,1024]{1,0:T(8,128)(2,1)S(1)}, u32[]{:S(2)}, u32[]{:S(2)}) collective-permute-start(bf16[256,1024]{1,0:T(8,128)(2,1)S(1)} %pad_maximum_fusion.3.refs_4_.refs_5_.refs_8_), channel_id=1, source_target_pairs={{0,16},{8,24},{16,0},{24,8},{1,17},{9,25},{17,1},{25,9},{2,18},{10... | collective-permute-start | bytes 1572872 | tf_op jit(solution)/shard_map/ppermute | solution.py:35
  28.5 22.3 %collective-permute-start.7 = (bf16[256,1024]{1,0:T(8,128)(2,1)S(1)}, bf16[256,1024]{1,0:T(8,128)(2,1)S(1)}, u32[]{:S(2)}, u32[]{:S(2)}) collective-permute-start(bf16[256,1024]{1,0:T(8,128)(2,1)S(1)} %pad_maximum_fusion.3.refs_4_.refs_5_.refs_8_), channel_id=1, source_target_pairs={{0,24},{8,16},{16,8},{24,0},{1,25},{9,17},{17,9},{25,1},{2,26},{10... | collective-permute-start | bytes 1572872 | tf_op jit(solution)/shard_map/ppermute | solution.py:35
  62.0 48.5 %collective-permute-start.9 = (bf16[128,2048]{1,0:T(8,128)(2,1)S(1)}, bf16[128,2048]{1,0:T(8,128)(2,1)S(1)}, u32[]{:S(2)}, u32[]{:S(2)}) collective-permute-start(bf16[128,2048]{1,0:T(8,128)(2,1)S(1)} %pad_maximum_fusion.4.refs_5_), channel_id=1, source_target_pairs={{0,4},{2,6},{4,0},{6,2},{1,5},{3,7},{5,1},{7,3},{8,12},{10,14},{12... | collective-permute-start | bytes 1572872 | tf_op jit(solution)/shard_map/ppermute | solution.py:35
  76.5 67.8 %collective-permute-start.13 = (bf16[1024,512]{1,0:T(8,128)(2,1)S(1)}, bf16[1024,512]{1,0:T(8,128)(2,1)S(1)}, u32[]{:S(2)}, u32[]{:S(2)}) collective-permute-start(bf16[1024,512]{1,0:T(8,128)(2,1)S(1)} %get-tuple-element.99), channel_id=1, source_target_pairs={{0,4},{2,6},{4,0},{6,2},{1,5},{3,7},{5,1},{7,3},{8,12},{10,14},{12... | collective-permute-start | bytes 3145736 | tf_op jit(solution)/shard_map/ppermute | solution.py:35
  110.7 52.1 %collective-permute-start.10 = (bf16[256,2048]{1,0:T(8,128)(2,1)S(1)}, bf16[256,2048]{1,0:T(8,128)(2,1)S(1)}, u32[]{:S(2)}, u32[]{:S(2)}) collective-permute-start(bf16[256,2048]{1,0:T(8,128)(2,1)S(1)} %constant_dynamic-update-slice_fusion.refs_9_.refs_5_), channel_id=1, source_target_pairs={{0,8},{8,0},{16,24},{24,16},{1,9},{9,1},{17,25},{25,17},{2,10},{10... | collective-permute-start | bytes 3145736 | tf_op jit(solution)/shard_map/ppermute | solution.py:35
  112.2 50.6 %collective-permute-start.11 = (bf16[256,2048]{1,0:T(8,128)(2,1)S(1)}, bf16[256,2048]{1,0:T(8,128)(2,1)S(1)}, u32[]{:S(2)}, u32[]{:S(2)}) collective-permute-start(bf16[256,2048]{1,0:T(8,128)(2,1)S(1)} %constant_dynamic-update-slice_fusion.refs_9_.refs_5_), channel_id=1, source_target_pairs={{0,16},{8,24},{16,0},{24,8},{1,17},{9,25},{17,1},{25,9},{2,18},{10... | collective-permute-start | bytes 3145736 | tf_op jit(solution)/shard_map/ppermute | solution.py:35
  113.7 49.1 %collective-permute-start.12 = (bf16[256,2048]{1,0:T(8,128)(2,1)S(1)}, bf16[256,2048]{1,0:T(8,128)(2,1)S(1)}, u32[]{:S(2)}, u32[]{:S(2)}) collective-permute-start(bf16[256,2048]{1,0:T(8,128)(2,1)S(1)} %constant_dynamic-update-slice_fusion.refs_9_.refs_5_), channel_id=1, source_target_pairs={{0,24},{8,16},{16,8},{24,0},{1,25},{9,17},{17,9},{25,1},{2,26},{10... | collective-permute-start | bytes 3145736 | tf_op jit(solution)/shard_map/ppermute | solution.py:35
  116.8 82.8 %collective-permute-start.18 = (bf16[512,512]{1,0:T(8,128)(2,1)}, bf16[512,512]{1,0:T(8,128)(2,1)}, u32[]{:S(2)}, u32[]{:S(2)}) collective-permute-start(bf16[512,512]{1,0:T(8,128)(2,1)} %get-tuple-element.111), channel_id=1, source_target_pairs={{0,4},{2,6},{4,0},{6,2},{1,5},{3,7},{5,1},{7,3},{8,12},{10,14},{12... | collective-permute-start | bytes 1572872 | tf_op jit(solution)/shard_map/ppermute | solution.py:35
  162.8 53.5 %collective-permute-start.17 = (bf16[1024,512]{1,0:T(8,128)(2,1)S(1)}, bf16[1024,512]{1,0:T(8,128)(2,1)S(1)}, u32[]{:S(2)}, u32[]{:S(2)}) collective-permute-start(bf16[1024,512]{1,0:T(8,128)(2,1)S(1)} %bitcast.110), channel_id=1, source_target_pairs={{0,4},{2,6},{4,0},{6,2},{1,5},{3,7},{5,1},{7,3},{8,12},{10,14},{12... | collective-permute-start | bytes 3145736 | tf_op jit(solution)/shard_map/ppermute | solution.py:35
  196.1 46.4 %collective-permute-start.14 = (bf16[2,256,1024]{2,1,0:T(8,128)(2,1)}, bf16[2,256,1024]{2,1,0:T(8,128)(2,1)}, u32[]{:S(2)}, u32[]{:S(2)}) collective-permute-start(bf16[2,256,1024]{2,1,0:T(8,128)(2,1)} %get-tuple-element.102), channel_id=1, source_target_pairs={{0,8},{8,0},{16,24},{24,16},{1,9},{9,1},{17,25},{25,17},{2,10},{10... | collective-permute-start | bytes 3145736 | tf_op jit(solution)/shard_map/ppermute | solution.py:35
  197.7 47.6 %collective-permute-start.15 = (bf16[2,256,1024]{2,1,0:T(8,128)(2,1)}, bf16[2,256,1024]{2,1,0:T(8,128)(2,1)}, u32[]{:S(2)}, u32[]{:S(2)}) collective-permute-start(bf16[2,256,1024]{2,1,0:T(8,128)(2,1)} %get-tuple-element.103), channel_id=1, source_target_pairs={{0,16},{8,24},{16,0},{24,8},{1,17},{9,25},{17,1},{25,9},{2,18},{10... | collective-permute-start | bytes 3145736 | tf_op jit(solution)/shard_map/ppermute | solution.py:35
  199.2 46.1 %collective-permute-start.16 = (bf16[2,256,1024]{2,1,0:T(8,128)(2,1)}, bf16[2,256,1024]{2,1,0:T(8,128)(2,1)}, u32[]{:S(2)}, u32[]{:S(2)}) collective-permute-start(bf16[2,256,1024]{2,1,0:T(8,128)(2,1)} %get-tuple-element.104), channel_id=1, source_target_pairs={{0,24},{8,16},{16,8},{24,0},{1,25},{9,17},{17,9},{25,1},{2,26},{10... | collective-permute-start | bytes 3145736 | tf_op jit(solution)/shard_map/ppermute | solution.py:35
  212.1 36.9 %collective-permute-start.21 = (bf16[512,512]{1,0:T(8,128)(2,1)}, bf16[512,512]{1,0:T(8,128)(2,1)S(1)}, u32[]{:S(2)}, u32[]{:S(2)}) collective-permute-start(bf16[512,512]{1,0:T(8,128)(2,1)} %bitcast.32), channel_id=1, source_target_pairs={{0,4},{2,6},{4,0},{6,2},{1,5},{3,7},{5,1},{7,3},{8,12},{10,14},{12... | collective-permute-start | bytes 1572872 | tf_op jit(solution)/shard_map/ppermute | solution.py:35
  232.7 34.4 %collective-permute-start.20 = (bf16[2,2,256,1024]{3,2,1,0:T(8,128)(2,1)}, bf16[2,2,256,1024]{3,2,1,0:T(8,128)(2,1)}, u32[]{:S(2)}, u32[]{:S(2)}) collective-permute-start(bf16[2,2,256,1024]{3,2,1,0:T(8,128)(2,1)} %get-tuple-element.117), channel_id=1, source_target_pairs={{0,1},{1,0},{2,3},{3,2},{4,5},{5,4},{6,7},{7,6},{8,9},{9,8},{10,11... | collective-permute-start | bytes 6291464 | tf_op jit(solution)/shard_map/ppermute | solution.py:35
  257.2 26.6 %collective-permute-start.19 = (bf16[2,128,1024]{2,1,0:T(8,128)(2,1)S(1)}, bf16[2,128,1024]{2,1,0:T(8,128)(2,1)S(1)}, u32[]{:S(2)}, u32[]{:S(2)}) collective-permute-start(bf16[2,128,1024]{2,1,0:T(8,128)(2,1)S(1)} %get-tuple-element.115), channel_id=1, source_target_pairs={{0,4},{2,6},{4,0},{6,2},{1,5},{3,7},{5,1},{7,3},{8,12},{10,14},{12... | collective-permute-start | bytes 1572872 | tf_op jit(solution)/shard_map/ppermute | solution.py:35
  263.6 21.7 %collective-permute-start.25 = (bf16[1,272,1024]{2,1,0:T(8,128)(2,1)S(1)}, bf16[1,272,1024]{2,1,0:T(8,128)(2,1)S(1)}, u32[]{:S(2)}, u32[]{:S(2)}) collective-permute-start(bf16[1,272,1024]{2,1,0:T(8,128)(2,1)S(1)} %get-tuple-element.124), channel_id=1, source_target_pairs={{0,8},{8,0},{16,24},{24,16},{1,9},{9,1},{17,25},{25,17},{2,10},{10... | collective-permute-start | bytes 1671176 | tf_op jit(solution)/shard_map/ppermute | solution.py:35
  264.9 24.7 %collective-permute-start.26 = (bf16[1,272,1024]{2,1,0:T(8,128)(2,1)S(1)}, bf16[1,272,1024]{2,1,0:T(8,128)(2,1)S(1)}, u32[]{:S(2)}, u32[]{:S(2)}) collective-permute-start(bf16[1,272,1024]{2,1,0:T(8,128)(2,1)S(1)} %get-tuple-element.125), channel_id=1, source_target_pairs={{0,16},{8,24},{16,0},{24,8},{1,17},{9,25},{17,1},{25,9},{2,18},{10... | collective-permute-start | bytes 1671176 | tf_op jit(solution)/shard_map/ppermute | solution.py:35
  265.7 25.5 %collective-permute-start.27 = (bf16[1,272,1024]{2,1,0:T(8,128)(2,1)S(1)}, bf16[1,272,1024]{2,1,0:T(8,128)(2,1)S(1)}, u32[]{:S(2)}, u32[]{:S(2)}) collective-permute-start(bf16[1,272,1024]{2,1,0:T(8,128)(2,1)S(1)} %get-tuple-element.126), channel_id=1, source_target_pairs={{0,24},{8,16},{16,8},{24,0},{1,25},{9,17},{17,9},{25,1},{2,26},{10... | collective-permute-start | bytes 1671176 | tf_op jit(solution)/shard_map/ppermute | solution.py:35
  269.5 59.5 %collective-permute-start.24 = (bf16[2,384,1024]{2,1,0:T(8,128)(2,1)}, bf16[2,384,1024]{2,1,0:T(8,128)(2,1)}, u32[]{:S(2)}, u32[]{:S(2)}) collective-permute-start(bf16[2,384,1024]{2,1,0:T(8,128)(2,1)} %core_sums.2.refs_2_), channel_id=1, source_target_pairs={{0,2},{2,0},{4,6},{6,4},{1,3},{3,1},{5,7},{7,5},{8,10},{10,8},{12,... | collective-permute-start | bytes 4718600 | tf_op jit(solution)/shard_map/ppermute | solution.py:35
  291.8 34.7 %collective-permute-start.28 = (bf16[1,80,1024]{2,1,0:T(8,128)(2,1)S(1)}, bf16[1,80,1024]{2,1,0:T(8,128)(2,1)S(1)}, u32[]{:S(2)}, u32[]{:S(2)}) collective-permute-start(bf16[1,80,1024]{2,1,0:T(8,128)(2,1)S(1)} %get-tuple-element.129), channel_id=1, source_target_pairs={{0,2},{2,0},{4,6},{6,4},{1,3},{3,1},{5,7},{7,5},{8,10},{10,8},{12,... | collective-permute-start | bytes 491528 | tf_op jit(solution)/shard_map/ppermute | solution.py:35
  292.3 34.3 %collective-permute-start.29 = (bf16[1,80,1024]{2,1,0:T(8,128)(2,1)S(1)}, bf16[1,80,1024]{2,1,0:T(8,128)(2,1)S(1)}, u32[]{:S(2)}, u32[]{:S(2)}) collective-permute-start(bf16[1,80,1024]{2,1,0:T(8,128)(2,1)S(1)} %get-tuple-element.130), channel_id=1, source_target_pairs={{0,4},{2,6},{4,0},{6,2},{1,5},{3,7},{5,1},{7,3},{8,12},{10,14},{12... | collective-permute-start | bytes 491528 | tf_op jit(solution)/shard_map/ppermute | solution.py:35
  294.9 31.7 %collective-permute-start.30 = (bf16[1,80,1024]{2,1,0:T(8,128)(2,1)S(1)}, bf16[1,80,1024]{2,1,0:T(8,128)(2,1)S(1)}, u32[]{:S(2)}, u32[]{:S(2)}) collective-permute-start(bf16[1,80,1024]{2,1,0:T(8,128)(2,1)S(1)} %get-tuple-element.131), channel_id=1, source_target_pairs={{0,6},{2,4},{4,2},{6,0},{1,7},{3,5},{5,3},{7,1},{8,14},{10,12},{12... | collective-permute-start | bytes 491528 | tf_op jit(solution)/shard_map/ppermute | solution.py:35
  296.3 43.0 %collective-permute-start.23 = (bf16[2,64,1024]{2,1,0:T(8,128)(2,1)}, bf16[2,64,1024]{2,1,0:T(8,128)(2,1)}, u32[]{:S(2)}, u32[]{:S(2)}) collective-permute-start(bf16[2,64,1024]{2,1,0:T(8,128)(2,1)} %get-tuple-element.123), channel_id=1, source_target_pairs={{0,2},{2,0},{4,6},{6,4},{1,3},{3,1},{5,7},{7,5},{8,10},{10,8},{12,... | collective-permute-start | bytes 786440 | tf_op jit(solution)/shard_map/ppermute | solution.py:35
  (79 other events, 855.7 us)

commit v2 on v1

--- a/solution.py
+++ b/solution.py
@@ -323,9 +323,9 @@
         for rank in range(blocks):
             rows = slice(rank * block_rows, (rank + 1) * block_rows)
             keys = slice(0, (rank + 1) * block_rows)
-            q_h = jnp.where(inside, q_s[rows, :], 0).astype(BF16)
+            q_h = (jnp.where(inside, q_s[rows, :], 0).astype(F32) * scale).astype(BF16)
             d_h = jnp.where(inside, d_s[rows, :], 0).astype(BF16)
-            scores = against(k_s[keys, :], q_h) * scale
+            scores = against(k_s[keys, :], q_h)
             weights = jnp.exp(scores - jnp.max(scores, axis=0, keepdims=True))
             weights = weights * (1.0 / jnp.sum(weights, axis=0, keepdims=True))
             low = weights.astype(BF16)
@@ -343,7 +343,7 @@
         rows, out, side = rows_of(index), out_refs[index // 2], index % 2
         cosine, sine = table_ref[0, rows, :], -table_ref[1, rows, :]
         out[side, 0, :, :LANES] = turn(qt_s[:, rows].T * scale, cosine, sine).astype(BF16)
-        out[side, 0, :, LANES : 2 * LANES] = turn(dk_s[rows, :] * scale, cosine, sine).astype(BF16)
+        out[side, 0, :, LANES : 2 * LANES] = turn(dk_s[rows, :], cosine, sine).astype(BF16)
         out[side, 0, :, 2 * LANES : 3 * LANES] = dv_s[rows, :].astype(BF16)
         out[side, 0, :, 3 * LANES :] = ot_s[:, rows].T.astype(BF16)
 

time: 347 us -> 347 us (level)
  no operation moved by 1% of the time
where the time goes in v2:
time: 347 us; the launch traced here: 343 us
  waiting for transfers between devices  132 us (38%)
  Pallas kernels  125 us (36%)
  starting transfers between devices  35.2 us (10%)
  local copies, waits for them, and re-layouts  31.2 us (9%)
  other arithmetic  17.6 us (5%)
    ppermute x33, waiting for transfers between devices, swap(): return lax.ppermute(value, axis, [(i, i ^ bit) for i in range(size)])  132 us
    pallas_call x18, Pallas kernels, launch(): pl.pallas_call(body, out_shape=out_shape, grid_spec=pltpu.PrefetchScalarG...  125 us
    ppermute x33, starting transfers between devices, swap(): return lax.ppermute(value, axis, [(i, i ^ bit) for i in range(size)])  35.2 us
    unnamed x145, local copies, waits for them, and re-layouts  26.1 us
  transfers between devices with their start and end apart: 33, of which 12 were waited for; matrix products, arithmetic and copies ran while one was open for 5% of the time, Pallas kernels for 36%

profile of v2, /device:TPU:0, one launch (start us, length us, event | category | flops | bytes accessed | tf_op | source)
XLA Modules:
  0.0 342.9 jit_solution(17283092124326721037)
XLA Ops:
  6.6 3.0 collective-permute-start
  20.0 4.2 %collective-permute-done.2 = bf16[64,1024]{1,0:T(8,128)(2,1)} collective-permute-done((bf16[64,1024]{1,0:T(8,128)(2,1)}, bf16[64,1024]{1,0:T(8,128)(2,1)}, u32[]{:S(2)}, u32[]{:S(2)}) %collective-permute-start.2) | collective-permute-done | bytes 131104 | tf_op jit(solution)/shard_map/ppermute | solution.py:35
  30.0 3.6 %prepare_own.1 = (bf16[768,1024]{1,0:T(8,128)(2,1)S(1)}, bf16[768,1024]{1,0:T(8,128)(2,1)S(1)}, bf16[768,1024]{1,0:T(8,128)(2,1)S(1)}, f32[1,1024]{1,0:T(1,128)S(1)}) custom-call(s32[2]{0:T(128)S(1)} %pad_add_fusion.refs_0_, bf16[768,1024]{1,0:T(8,128)(2,1)S(1)} %bitcast.99, bf16[768,1024]{1,0:T(8,128)(2,1)S(1)} %bitcast.102, ...), custom_call_target="tpu_custom_call" | custom-call | flops 3849999872 | bytes 1024 | tf_op jit(solution)/shard_map/prepare_own/pallas_call | solution.py:56
  37.2 3.2 collective-permute-done.5.refs_6_.refs_9_
  40.4 10.5 %collective-permute-done.6.refs_7_.refs_10_ = bf16[256,1024]{1,0:T(8,128)(2,1)S(1)} collective-permute-done((bf16[256,1024]{1,0:T(8,128)(2,1)S(1)}, bf16[256,1024]{1,0:T(8,128)(2,1)S(1)}, u32[]{:S(2)}, u32[]{:S(2)}) %collective-permute-start.6) | collective-permute-done | bytes 524320 | tf_op jit(solution)/shard_map/ppermute | solution.py:35
  51.7 8.3 %collective-permute-done.1.refs_1_ = bf16[2,768,512]{2,1,0:T(8,128)(2,1)} collective-permute-done((bf16[2,768,512]{2,1,0:T(8,128)(2,1)}, bf16[2,768,512]{2,1,0:T(8,128)(2,1)}, u32[]{:S(2)}, u32[]{:S(2)}) %collective-permute-start.1) | collective-permute-done | bytes 1572896 | tf_op jit(solution)/shard_map/ppermute | solution.py:35
  68.0 5.3 %prepare_pair.1 = (bf16[1536,1024]{1,0:T(8,128)(2,1)S(1)}, bf16[1536,1024]{1,0:T(8,128)(2,1)S(1)}, bf16[1536,1024]{1,0:T(8,128)(2,1)S(1)}) custom-call(s32[2]{0:T(128)S(1)} %pad_add_fusion.refs_0_, bf16[2,768,512]{2,1,0:T(8,128)(2,1)} %collective-permute-done.1.refs_1_, bf16[2,768,512]{2,1,0:T(8,128)(2,1)} %collective-permute-done.8.refs_2_, ...), custom_call_target="tpu_custom_call" | custom-call | flops 3849999872 | bytes 1024 | tf_op jit(solution)/shard_map/prepare_pair/pallas_call | solution.py:56
  73.3 3.2 project.2
  77.9 32.7 %collective-permute-done.9 = bf16[128,2048]{1,0:T(8,128)(2,1)S(1)} collective-permute-done((bf16[128,2048]{1,0:T(8,128)(2,1)S(1)}, bf16[128,2048]{1,0:T(8,128)(2,1)S(1)}, u32[]{:S(2)}, u32[]{:S(2)}) %collective-permute-start.9) | collective-permute-done | bytes 524320 | tf_op jit(solution)/shard_map/ppermute | solution.py:35
  116.9 5.9 %prepare_late.1 = (bf16[1536,1024]{1,0:T(8,128)(2,1)S(1)}, bf16[1024,1536]{1,0:T(8,128)(2,1)S(1)}, bf16[1024,1536]{1,0:T(8,128)(2,1)S(1)}, bf16[1024,1536]{1,0:T(8,128)(2,1)S(1)}) custom-call(s32[2]{0:T(128)S(1)} %pad_add_fusion.refs_0_, bf16[1536,1024]{1,0:T(8,128)(2,1)S(1)} %get-tuple-element.85.refs_1_, ...), custom_call_target="tpu_custom_call" | custom-call | flops 6600000000 | bytes 1024 | tf_op jit(solution)/shard_map/prepare_late/pallas_call | solution.py:56
  124.4 19.9 %collective-permute-done.13 = bf16[1024,512]{1,0:T(8,128)(2,1)S(1)} collective-permute-done((bf16[1024,512]{1,0:T(8,128)(2,1)S(1)}, bf16[1024,512]{1,0:T(8,128)(2,1)S(1)}, u32[]{:S(2)}, u32[]{:S(2)}) %collective-permute-start.13) | collective-permute-done | bytes 1048608 | tf_op jit(solution)/shard_map/ppermute | solution.py:35
  144.3 17.6 %attend.2 = (bf16[2,2,256,512]{3,2,1,0:T(8,128)(2,1)S(1)}, bf16[2,2,256,512]{3,2,1,0:T(8,128)(2,1)S(1)}) custom-call(s32[8]{0:T(128)S(1)} %reshape.372.refs_0_, f32[2,1024,128]{2,1,0:T(8,128)S(1)} %pad_maximum_fusion.1.refs_6_.refs_3_.refs_1_, bf16[2,2,256,512]{3,2,1,0:T(8,128)(2,1)S(1)} %bitcast.113, bf16[2,2,256,512]{3,2,1,0:T(8,128)(2,1)S(1)} %bitcast.111, ...), custom_call_target="tpu_custom_call" | custom-call | flops 40333332480 | bytes 1024 | tf_op jit(solution)/shard_map/attend/pallas_call | solution.py:56
  164.9 31.4 %feed_forward.1 = (f32[1536,1024]{1,0:T(8,128)}, f32[1536,1024]{1,0:T(8,128)}, f32[1,1024]{1,0:T(1,128)}, f32[2,256,1024]{2,1,0:T(8,128)}, bf16[2,256,1024]{2,1,...) custom-call(bf16[1536,1024]{1,0:T(8,128)(2,1)} %copy-done.51, ...), custom_call_target="tpu_custom_call" | custom-call | flops 62333333504 | bytes 1024 | tf_op jit(solution)/shard_map/feed_forward/pallas_call | solution.py:56
  200.5 11.2 %attend.3 = (bf16[2,1,256,512]{3,2,1,0:T(8,128)(2,1)S(1)}, bf16[2,1,256,512]{3,2,1,0:T(8,128)(2,1)}) custom-call(s32[4]{0:T(128)S(1)} %select_reduce_fusion.1.refs_0_, f32[2,1024,128]{2,1,0:T(8,128)S(1)} %pad_maximum_fusion.1.refs_6_.refs_3_.refs_1_, bf16[2,1,256,512]{3,2,1,0:T(8,128)(2,1)S(1)} %bitcast.112, bf16[2,1,256,512]{3,2,1,0:T(8,128)(2,1)} %bitcast.30.refs_3_, ...), custom_call_target="tpu_custom_call" | custom-call | flops 20166666240 | bytes 1024 | tf_op jit(solution)/shard_map/attend/pallas_call | solution.py:56
  212.5 2.9 collective-permute-start.21
  217.7 15.4 %finish.2 = (bf16[2,2,256,1024]{3,2,1,0:T(8,128)(2,1)}, bf16[2,2,256,1024]{3,2,1,0:T(8,128)(2,1)}, f32[16,1024]{1,0:T(8,128)}) custom-call(s32[4]{0:T(128)} %pad_add_fusion.3.refs_0_, bf16[1536,1024]{1,0:T(8,128)(2,1)} %copy-done.6, f32[4,1024]{1,0:T(4,128)} %copy-done.33, f32[1536,1024]{1,0:T(8,128)} %get-tuple-element.107.refs_3_, ...), custom_call_target="tpu_custom_call" | custom-call | flops 916666688 | bytes 1024 | tf_op jit(solution)/shard_map/finish/pallas_call | solution.py:56
  239.0 3.8 %attention_weights.2.refs_4_.refs_5_ = f32[4,256,1024]{2,1,0:T(8,128)S(1)} custom-call(s32[1]{0:T(128)} %bitcast.19.refs_0_, bf16[1024,1536]{1,0:T(8,128)(2,1)S(1)} %copy-done.9, bf16[1024,1536]{1,0:T(8,128)(2,1)S(1)} %copy-done.12, bf16[1024,512]{1,0:T(8,128)(2,1)S(1)} %bitcast.97, bf16[1024,512]{1,0:T(8,128)(2,1)S(1)} %copy-done.5, f32[16,1024]{1,0:T(8,128)S(1)} %copy-done.31), custom_call_target="tpu_custom_call" | custom-call | flops 916666688 | bytes 1024 | tf_op jit(solution)/shard_map/attention_weights/pallas_call | solution.py:56
  245.5 3.6 %reduce_and_cut.3 = (f32[2,128,1024]{2,1,0:T(8,128)S(1)}, bf16[2,128,1024]{2,1,0:T(8,128)(2,1)S(1)}) custom-call(f32[2,256,1024]{2,1,0:T(8,128)S(1)} %copy-done.50, bf16[2,256,1024]{2,1,0:T(8,128)(2,1)} %collective-permute-done.14.refs_1_, bf16[2,256,1024]{2,1,0:T(8,128)(2,1)} %collective-permute-done.15.refs_2_, ...), custom_call_target="tpu_custom_call" | custom-call | flops 5500000256 | bytes 1024 | tf_op jit(solution)/shard_map/reduce_and_cut/pallas_call | solution.py:56
  249.3 7.8 %finish.3 = (bf16[2,2,128,1024]{3,2,1,0:T(8,128)(2,1)S(1)}, bf16[2,2,128,1024]{3,2,1,0:T(8,128)(2,1)S(1)}, f32[16,1024]{1,0:T(8,128)S(1)}) custom-call(s32[4]{0:T(128)S(1)} %copy-done.36, bf16[1536,1024]{1,0:T(8,128)(2,1)S(1)} %copy-done.7, f32[4,1024]{1,0:T(4,128)S(1)} %copy-done.34, f32[1536,1024]{1,0:T(8,128)} %get-tuple-element.107.refs_3_, ...), custom_call_target="tpu_custom_call" | custom-call | flops 11733332992 | bytes 1024 | tf_op jit(solution)/shard_map/finish/pallas_call | solution.py:56
  257.2 2.7 collective-permute-start.19
  269.9 13.9 %collective-permute-done.19.refs_1_ = bf16[2,128,1024]{2,1,0:T(8,128)(2,1)S(1)} collective-permute-done((bf16[2,128,1024]{2,1,0:T(8,128)(2,1)S(1)}, bf16[2,128,1024]{2,1,0:T(8,128)(2,1)S(1)}, u32[]{:S(2)}, u32[]{:S(2)}) %collective-permute-start.19) | collective-permute-done | bytes 524320 | tf_op jit(solution)/shard_map/ppermute | solution.py:35
  285.3 4.3 %collective-permute-done.26.refs_2_ = bf16[1,272,1024]{2,1,0:T(8,128)(2,1)S(1)} collective-permute-done((bf16[1,272,1024]{2,1,0:T(8,128)(2,1)S(1)}, bf16[1,272,1024]{2,1,0:T(8,128)(2,1)S(1)}, u32[]{:S(2)}, u32[]{:S(2)}) %collective-permute-start.26) | collective-permute-done | bytes 557088 | tf_op jit(solution)/shard_map/ppermute | solution.py:35
  296.3 30.2 %collective-permute-done.28.refs_6_ = bf16[1,80,1024]{2,1,0:T(8,128)(2,1)S(1)} collective-permute-done((bf16[1,80,1024]{2,1,0:T(8,128)(2,1)S(1)}, bf16[1,80,1024]{2,1,0:T(8,128)(2,1)S(1)}, u32[]{:S(2)}, u32[]{:S(2)}) %collective-permute-start.28) | collective-permute-done | bytes 163872 | tf_op jit(solution)/shard_map/ppermute | solution.py:35
  335.0 4.3 %close.1 = (bf16[768,1024]{1,0:T(8,128)(2,1)}, bf16[768,1024]{1,0:T(8,128)(2,1)}) custom-call(s32[1]{0:T(128)} %bitcast.1.refs_0_, bf16[768,1024]{1,0:T(8,128)(2,1)S(1)} %bitcast.100, bf16[768,1024]{1,0:T(8,128)(2,1)S(1)} %bitcast.103, bf16[2,384,1024]{2,1,0:T(8,128)(2,1)S(1)} %core_sums.3.refs_3_.refs_6_, ...), custom_call_target="tpu_custom_call" | custom-call | flops 5500000256 | bytes 1024 | tf_op jit(solution)/shard_map/close/pallas_call | solution.py:56
  (283 shorter events, 91.9 us)
Async XLA Ops:
  17.1 42.9 %collective-permute-start.1 = (bf16[2,768,512]{2,1,0:T(8,128)(2,1)}, bf16[2,768,512]{2,1,0:T(8,128)(2,1)}, u32[]{:S(2)}, u32[]{:S(2)}) collective-permute-start(bf16[2,768,512]{2,1,0:T(8,128)(2,1)} %slice_select_fusion), channel_id=1, source_target_pairs={{0,2},{2,0},{4,6},{6,4},{1,3},{3,1},{5,7},{7,5},{8,10},{10,8},{12,... | collective-permute-start | bytes 4718600 | tf_op jit(solution)/shard_map/ppermute | solution.py:35
  27.0 23.9 %collective-permute-start.6 = (bf16[256,1024]{1,0:T(8,128)(2,1)S(1)}, bf16[256,1024]{1,0:T(8,128)(2,1)S(1)}, u32[]{:S(2)}, u32[]{:S(2)}) collective-permute-start(bf16[256,1024]{1,0:T(8,128)(2,1)S(1)} %pad_maximum_fusion.3.refs_4_.refs_5_.refs_8_), channel_id=1, source_target_pairs={{0,16},{8,24},{16,0},{24,8},{1,17},{9,25},{17,1},{25,9},{2,18},{10... | collective-permute-start | bytes 1572872 | tf_op jit(solution)/shard_map/ppermute | solution.py:35
  28.5 22.3 %collective-permute-start.7 = (bf16[256,1024]{1,0:T(8,128)(2,1)S(1)}, bf16[256,1024]{1,0:T(8,128)(2,1)S(1)}, u32[]{:S(2)}, u32[]{:S(2)}) collective-permute-start(bf16[256,1024]{1,0:T(8,128)(2,1)S(1)} %pad_maximum_fusion.3.refs_4_.refs_5_.refs_8_), channel_id=1, source_target_pairs={{0,24},{8,16},{16,8},{24,0},{1,25},{9,17},{17,9},{25,1},{2,26},{10... | collective-permute-start | bytes 1572872 | tf_op jit(solution)/shard_map/ppermute | solution.py:35
  62.0 48.5 %collective-permute-start.9 = (bf16[128,2048]{1,0:T(8,128)(2,1)S(1)}, bf16[128,2048]{1,0:T(8,128)(2,1)S(1)}, u32[]{:S(2)}, u32[]{:S(2)}) collective-permute-start(bf16[128,2048]{1,0:T(8,128)(2,1)S(1)} %pad_maximum_fusion.4.refs_5_), channel_id=1, source_target_pairs={{0,4},{2,6},{4,0},{6,2},{1,5},{3,7},{5,1},{7,3},{8,12},{10,14},{12... | collective-permute-start | bytes 1572872 | tf_op jit(solution)/shard_map/ppermute | solution.py:35
  76.5 67.8 %collective-permute-start.13 = (bf16[1024,512]{1,0:T(8,128)(2,1)S(1)}, bf16[1024,512]{1,0:T(8,128)(2,1)S(1)}, u32[]{:S(2)}, u32[]{:S(2)}) collective-permute-start(bf16[1024,512]{1,0:T(8,128)(2,1)S(1)} %get-tuple-element.99), channel_id=1, source_target_pairs={{0,4},{2,6},{4,0},{6,2},{1,5},{3,7},{5,1},{7,3},{8,12},{10,14},{12... | collective-permute-start | bytes 3145736 | tf_op jit(solution)/shard_map/ppermute | solution.py:35
  110.7 52.3 %collective-permute-start.10 = (bf16[256,2048]{1,0:T(8,128)(2,1)S(1)}, bf16[256,2048]{1,0:T(8,128)(2,1)S(1)}, u32[]{:S(2)}, u32[]{:S(2)}) collective-permute-start(bf16[256,2048]{1,0:T(8,128)(2,1)S(1)} %constant_dynamic-update-slice_fusion.refs_9_.refs_5_), channel_id=1, source_target_pairs={{0,8},{8,0},{16,24},{24,16},{1,9},{9,1},{17,25},{25,17},{2,10},{10... | collective-permute-start | bytes 3145736 | tf_op jit(solution)/shard_map/ppermute | solution.py:35
  112.2 50.7 %collective-permute-start.11 = (bf16[256,2048]{1,0:T(8,128)(2,1)S(1)}, bf16[256,2048]{1,0:T(8,128)(2,1)S(1)}, u32[]{:S(2)}, u32[]{:S(2)}) collective-permute-start(bf16[256,2048]{1,0:T(8,128)(2,1)S(1)} %constant_dynamic-update-slice_fusion.refs_9_.refs_5_), channel_id=1, source_target_pairs={{0,16},{8,24},{16,0},{24,8},{1,17},{9,25},{17,1},{25,9},{2,18},{10... | collective-permute-start | bytes 3145736 | tf_op jit(solution)/shard_map/ppermute | solution.py:35
  113.7 49.2 %collective-permute-start.12 = (bf16[256,2048]{1,0:T(8,128)(2,1)S(1)}, bf16[256,2048]{1,0:T(8,128)(2,1)S(1)}, u32[]{:S(2)}, u32[]{:S(2)}) collective-permute-start(bf16[256,2048]{1,0:T(8,128)(2,1)S(1)} %constant_dynamic-update-slice_fusion.refs_9_.refs_5_), channel_id=1, source_target_pairs={{0,24},{8,16},{16,8},{24,0},{1,25},{9,17},{17,9},{25,1},{2,26},{10... | collective-permute-start | bytes 3145736 | tf_op jit(solution)/shard_map/ppermute | solution.py:35
  116.8 83.0 %collective-permute-start.18 = (bf16[512,512]{1,0:T(8,128)(2,1)}, bf16[512,512]{1,0:T(8,128)(2,1)}, u32[]{:S(2)}, u32[]{:S(2)}) collective-permute-start(bf16[512,512]{1,0:T(8,128)(2,1)} %get-tuple-element.111), channel_id=1, source_target_pairs={{0,4},{2,6},{4,0},{6,2},{1,5},{3,7},{5,1},{7,3},{8,12},{10,14},{12... | collective-permute-start | bytes 1572872 | tf_op jit(solution)/shard_map/ppermute | solution.py:35
  162.9 53.8 %collective-permute-start.17 = (bf16[1024,512]{1,0:T(8,128)(2,1)S(1)}, bf16[1024,512]{1,0:T(8,128)(2,1)S(1)}, u32[]{:S(2)}, u32[]{:S(2)}) collective-permute-start(bf16[1024,512]{1,0:T(8,128)(2,1)S(1)} %bitcast.110), channel_id=1, source_target_pairs={{0,4},{2,6},{4,0},{6,2},{1,5},{3,7},{5,1},{7,3},{8,12},{10,14},{12... | collective-permute-start | bytes 3145736 | tf_op jit(solution)/shard_map/ppermute | solution.py:35
  196.3 46.6 %collective-permute-start.14 = (bf16[2,256,1024]{2,1,0:T(8,128)(2,1)}, bf16[2,256,1024]{2,1,0:T(8,128)(2,1)}, u32[]{:S(2)}, u32[]{:S(2)}) collective-permute-start(bf16[2,256,1024]{2,1,0:T(8,128)(2,1)} %get-tuple-element.102), channel_id=1, source_target_pairs={{0,8},{8,0},{16,24},{24,16},{1,9},{9,1},{17,25},{25,17},{2,10},{10... | collective-permute-start | bytes 3145736 | tf_op jit(solution)/shard_map/ppermute | solution.py:35
  197.8 47.6 %collective-permute-start.15 = (bf16[2,256,1024]{2,1,0:T(8,128)(2,1)}, bf16[2,256,1024]{2,1,0:T(8,128)(2,1)}, u32[]{:S(2)}, u32[]{:S(2)}) collective-permute-start(bf16[2,256,1024]{2,1,0:T(8,128)(2,1)} %get-tuple-element.103), channel_id=1, source_target_pairs={{0,16},{8,24},{16,0},{24,8},{1,17},{9,25},{17,1},{25,9},{2,18},{10... | collective-permute-start | bytes 3145736 | tf_op jit(solution)/shard_map/ppermute | solution.py:35
  199.3 46.1 %collective-permute-start.16 = (bf16[2,256,1024]{2,1,0:T(8,128)(2,1)}, bf16[2,256,1024]{2,1,0:T(8,128)(2,1)}, u32[]{:S(2)}, u32[]{:S(2)}) collective-permute-start(bf16[2,256,1024]{2,1,0:T(8,128)(2,1)} %get-tuple-element.104), channel_id=1, source_target_pairs={{0,24},{8,16},{16,8},{24,0},{1,25},{9,17},{17,9},{25,1},{2,26},{10... | collective-permute-start | bytes 3145736 | tf_op jit(solution)/shard_map/ppermute | solution.py:35
  212.5 36.7 %collective-permute-start.21 = (bf16[512,512]{1,0:T(8,128)(2,1)}, bf16[512,512]{1,0:T(8,128)(2,1)S(1)}, u32[]{:S(2)}, u32[]{:S(2)}) collective-permute-start(bf16[512,512]{1,0:T(8,128)(2,1)} %bitcast.32), channel_id=1, source_target_pairs={{0,4},{2,6},{4,0},{6,2},{1,5},{3,7},{5,1},{7,3},{8,12},{10,14},{12... | collective-permute-start | bytes 1572872 | tf_op jit(solution)/shard_map/ppermute | solution.py:35
  233.1 34.0 %collective-permute-start.20 = (bf16[2,2,256,1024]{3,2,1,0:T(8,128)(2,1)}, bf16[2,2,256,1024]{3,2,1,0:T(8,128)(2,1)}, u32[]{:S(2)}, u32[]{:S(2)}) collective-permute-start(bf16[2,2,256,1024]{3,2,1,0:T(8,128)(2,1)} %get-tuple-element.117), channel_id=1, source_target_pairs={{0,1},{1,0},{2,3},{3,2},{4,5},{5,4},{6,7},{7,6},{8,9},{9,8},{10,11... | collective-permute-start | bytes 6291464 | tf_op jit(solution)/shard_map/ppermute | solution.py:35
  257.2 26.6 %collective-permute-start.19 = (bf16[2,128,1024]{2,1,0:T(8,128)(2,1)S(1)}, bf16[2,128,1024]{2,1,0:T(8,128)(2,1)S(1)}, u32[]{:S(2)}, u32[]{:S(2)}) collective-permute-start(bf16[2,128,1024]{2,1,0:T(8,128)(2,1)S(1)} %get-tuple-element.115), channel_id=1, source_target_pairs={{0,4},{2,6},{4,0},{6,2},{1,5},{3,7},{5,1},{7,3},{8,12},{10,14},{12... | collective-permute-start | bytes 1572872 | tf_op jit(solution)/shard_map/ppermute | solution.py:35
  263.6 21.7 %collective-permute-start.25 = (bf16[1,272,1024]{2,1,0:T(8,128)(2,1)S(1)}, bf16[1,272,1024]{2,1,0:T(8,128)(2,1)S(1)}, u32[]{:S(2)}, u32[]{:S(2)}) collective-permute-start(bf16[1,272,1024]{2,1,0:T(8,128)(2,1)S(1)} %get-tuple-element.124), channel_id=1, source_target_pairs={{0,8},{8,0},{16,24},{24,16},{1,9},{9,1},{17,25},{25,17},{2,10},{10... | collective-permute-start | bytes 1671176 | tf_op jit(solution)/shard_map/ppermute | solution.py:35
  264.8 24.7 %collective-permute-start.26 = (bf16[1,272,1024]{2,1,0:T(8,128)(2,1)S(1)}, bf16[1,272,1024]{2,1,0:T(8,128)(2,1)S(1)}, u32[]{:S(2)}, u32[]{:S(2)}) collective-permute-start(bf16[1,272,1024]{2,1,0:T(8,128)(2,1)S(1)} %get-tuple-element.125), channel_id=1, source_target_pairs={{0,16},{8,24},{16,0},{24,8},{1,17},{9,25},{17,1},{25,9},{2,18},{10... | collective-permute-start | bytes 1671176 | tf_op jit(solution)/shard_map/ppermute | solution.py:35
  265.7 25.5 %collective-permute-start.27 = (bf16[1,272,1024]{2,1,0:T(8,128)(2,1)S(1)}, bf16[1,272,1024]{2,1,0:T(8,128)(2,1)S(1)}, u32[]{:S(2)}, u32[]{:S(2)}) collective-permute-start(bf16[1,272,1024]{2,1,0:T(8,128)(2,1)S(1)} %get-tuple-element.126), channel_id=1, source_target_pairs={{0,24},{8,16},{16,8},{24,0},{1,25},{9,17},{17,9},{25,1},{2,26},{10... | collective-permute-start | bytes 1671176 | tf_op jit(solution)/shard_map/ppermute | solution.py:35
  269.5 59.5 %collective-permute-start.24 = (bf16[2,384,1024]{2,1,0:T(8,128)(2,1)}, bf16[2,384,1024]{2,1,0:T(8,128)(2,1)}, u32[]{:S(2)}, u32[]{:S(2)}) collective-permute-start(bf16[2,384,1024]{2,1,0:T(8,128)(2,1)} %core_sums.2.refs_2_), channel_id=1, source_target_pairs={{0,2},{2,0},{4,6},{6,4},{1,3},{3,1},{5,7},{7,5},{8,10},{10,8},{12,... | collective-permute-start | bytes 4718600 | tf_op jit(solution)/shard_map/ppermute | solution.py:35
  291.8 34.8 %collective-permute-start.28 = (bf16[1,80,1024]{2,1,0:T(8,128)(2,1)S(1)}, bf16[1,80,1024]{2,1,0:T(8,128)(2,1)S(1)}, u32[]{:S(2)}, u32[]{:S(2)}) collective-permute-start(bf16[1,80,1024]{2,1,0:T(8,128)(2,1)S(1)} %get-tuple-element.129), channel_id=1, source_target_pairs={{0,2},{2,0},{4,6},{6,4},{1,3},{3,1},{5,7},{7,5},{8,10},{10,8},{12,... | collective-permute-start | bytes 491528 | tf_op jit(solution)/shard_map/ppermute | solution.py:35
  292.2 34.4 %collective-permute-start.29 = (bf16[1,80,1024]{2,1,0:T(8,128)(2,1)S(1)}, bf16[1,80,1024]{2,1,0:T(8,128)(2,1)S(1)}, u32[]{:S(2)}, u32[]{:S(2)}) collective-permute-start(bf16[1,80,1024]{2,1,0:T(8,128)(2,1)S(1)} %get-tuple-element.130), channel_id=1, source_target_pairs={{0,4},{2,6},{4,0},{6,2},{1,5},{3,7},{5,1},{7,3},{8,12},{10,14},{12... | collective-permute-start | bytes 491528 | tf_op jit(solution)/shard_map/ppermute | solution.py:35
  294.9 31.8 %collective-permute-start.30 = (bf16[1,80,1024]{2,1,0:T(8,128)(2,1)S(1)}, bf16[1,80,1024]{2,1,0:T(8,128)(2,1)S(1)}, u32[]{:S(2)}, u32[]{:S(2)}) collective-permute-start(bf16[1,80,1024]{2,1,0:T(8,128)(2,1)S(1)} %get-tuple-element.131), channel_id=1, source_target_pairs={{0,6},{2,4},{4,2},{6,0},{1,7},{3,5},{5,3},{7,1},{8,14},{10,12},{12... | collective-permute-start | bytes 491528 | tf_op jit(solution)/shard_map/ppermute | solution.py:35
  296.2 43.1 %collective-permute-start.23 = (bf16[2,64,1024]{2,1,0:T(8,128)(2,1)}, bf16[2,64,1024]{2,1,0:T(8,128)(2,1)}, u32[]{:S(2)}, u32[]{:S(2)}) collective-permute-start(bf16[2,64,1024]{2,1,0:T(8,128)(2,1)} %get-tuple-element.123), channel_id=1, source_target_pairs={{0,2},{2,0},{4,6},{6,4},{1,3},{3,1},{5,7},{7,5},{8,10},{10,8},{12,... | collective-permute-start | bytes 786440 | tf_op jit(solution)/shard_map/ppermute | solution.py:35
  (79 other events, 855.3 us)
